TPU v7x, 256 devices: a whole 4x4x8 slice. The times are simulated.
256 devices in a mesh: cfg: 2 (over x_lo), wide: 32 (over x_hi, z, core), narrow: 4 (over y).
Axes of the slice: x: 4 (x_hi: 2, x_lo: 2; x = x_hi * 2 + x_lo), y: 4, z: 8, core: 2. Of those that a mesh axis runs over, the one named last changes fastest.
Arguments:
- hidden: bfloat16 [2, 4096, 3072], P('cfg', 'wide', 'narrow'), may hold values from -120 to 120
- split_table: int32 [32], replicated, may hold values from 1 to 128, 2048 in all
- modulation: float32 [8, 3072], P(None, 'narrow'), may hold values from -4 to 4
- expand_weight: bfloat16 [3072, 12288], P('narrow', 'wide'), may hold values from -0.109375 to 0.109375
- contract_weight: bfloat16 [12288, 3072], P('wide', 'narrow'), may hold values from -0.0546875 to 0.0546875
- output_weight: bfloat16 [3072, 64], P('narrow'), may hold values from -0.109375 to 0.109375
- latent: float32 [4096, 64], P('wide'), may hold values from -6 to 6
- timestep: int32 [1], replicated, may hold values from 20 to 499
Outputs:
- layer_out: bfloat16 [2, 4096, 3072], P('cfg', 'wide', 'narrow')
- clean_latent: float32 [4096, 64], P('wide')
Inputs may be any that keep to these rules, and one draw needn't show every extreme that they name: `split_table`: the entries sum to 2048, and the largest is exactly 128.
All inputs are finite; a program needn't handle non-finite values.
Results may differ from a plain program's by a relative error of at most 0.0056.
Values may be sent and summed in bfloat16 or wider, within the bound.
A program may use at most 64 MiB of HBM per device.

v0:
```python
import jax
import jax.numpy as jnp
from jax import lax
from jax.sharding import PartitionSpec as P

D = 3072
TEXT = 226


norm_eps = 1e-05
guidance = 6.0


def alpha_table():
    steps_index = jnp.arange(1000, dtype=jnp.int32)
    start_root = 0.00085**0.5
    end_root = 0.012**0.5
    roots = start_root + (end_root - start_root) * steps_index.astype(jnp.float32) / 999.0
    return (steps_index, jnp.cumprod(1.0 - roots * roots))


def feature_norm(values, shifts, scaling):
    totals, squares = lax.psum(
        (jnp.sum(values, -1, keepdims=True), jnp.sum(values * values, -1, keepdims=True)), "narrow"
    )
    average = totals / D
    variance = squares / D - average * average
    return (values - average) * lax.rsqrt(variance + norm_eps) * (1.0 + scaling) + shifts


def on_device(
    hidden, split_table, modulation, expand_weight, contract_weight, output_weight, latent, timestep
):
    capacity = hidden.shape[1]
    wide_index = lax.axis_index("wide")
    table_index = jnp.arange(split_table.shape[0], dtype=jnp.int32)
    offset = jnp.sum(jnp.where(table_index < wide_index, split_table, 0))
    own_count = jnp.sum(jnp.where(table_index == wide_index, split_table, 0))
    slot_index = jnp.arange(capacity, dtype=jnp.int32)
    position = offset + slot_index
    slot_live = slot_index < own_count
    is_text = slot_live & (position < TEXT)
    is_video = slot_live & (position >= TEXT)
    text_column = is_text[:, None]
    shifts = jnp.where(text_column, modulation[3], modulation[0])
    scaling = jnp.where(text_column, modulation[4], modulation[1])
    gating = jnp.where(text_column, modulation[5], modulation[2])
    values = hidden[0].astype(jnp.float32)
    normed = feature_norm(values, shifts, scaling).astype(jnp.bfloat16)
    hidden_part = jnp.dot(
        lax.all_gather(normed, "wide", axis=0, tiled=True),
        expand_weight,
        preferred_element_type=jnp.float32,
    )
    hidden_pre = lax.psum(hidden_part, "narrow")
    activated = jax.nn.gelu(hidden_pre, approximate=True).astype(jnp.bfloat16)
    ff_result = lax.psum_scatter(
        jnp.dot(activated, contract_weight, preferred_element_type=jnp.float32),
        "wide",
        scatter_dimension=0,
        tiled=True,
    )
    layer_out = jnp.where(slot_live[:, None], values + gating * ff_result, 0.0).astype(jnp.bfloat16)
    final_in = layer_out.astype(jnp.float32)
    final_normed = feature_norm(final_in, modulation[6], modulation[7]).astype(jnp.bfloat16)
    velocity_part = jnp.dot(final_normed, output_weight, preferred_element_type=jnp.float32)
    copy_weight = jnp.where(lax.axis_index("cfg") == 0, guidance, 1.0 - guidance)
    guided = lax.psum(velocity_part * copy_weight, ("cfg", "narrow"))
    steps_index, alpha_bar = alpha_table()
    alpha_now = jnp.sum(jnp.where(steps_index == timestep[0], alpha_bar, 0.0))
    clean_latent = jnp.where(
        is_video[:, None], jnp.sqrt(alpha_now) * latent - jnp.sqrt(1.0 - alpha_now) * guided, 0.0
    )
    return (layer_out[None], clean_latent)


def solution(mesh):
    return jax.shard_map(
        on_device,
        mesh=mesh,
        in_specs=(
            P("cfg", "wide", "narrow"),
            P(),
            P(None, "narrow"),
            P("narrow", "wide"),
            P("wide", "narrow"),
            P("narrow", None),
            P("wide", None),
            P(),
        ),
        out_specs=(P("cfg", "wide", "narrow"), P("wide", None)),
        check_vma=False,
    )
```

profile of v0, /device:TPU:2, one launch (start us, length us, event | category | flops | bytes accessed | tf_op | source)
XLA Modules:
  0.0 493.6 jit_solution(13559903819700724804)
XLA Ops:
  7.2 0.0 copy-start
  7.2 0.0 all-gather.2.cloned.1.call-start
  7.2 1.1 convert_reduce_fusion.1
  8.3 1.1 fusion.21
  9.4 1.1 add_reduce_fusion
  10.5 1.3 fusion.34
  11.8 1.3 compare_and_fusion.1
  13.1 10.7 %all-reduce.2 = (f32[128,1]{0,1:T(1,128)S(1)}, f32[128,1]{0,1:T(1,128)S(1)}) all-reduce(f32[128,1]{0,1:T(1,128)S(1)} %bitcast.48, f32[128,1]{0,1:T(1,128)S(1)} %bitcast.47), channel_id=1, replica_groups=mesh['cfg'=2,'wide'=32,'narrow'=4] {'narrow'}, use_global_device_ids=true, to_apply=%region_5.6 | all-reduce | flops 256 | bytes 2048 | tf_op jit(solution)/shard_map/psum | solution.py:23
  23.8 1.8 fusion.20
  25.7 0.0 all-gather.2.cloned.1.call-update
  25.7 0.0 all-reduce.5.cloned.1.call-start
  25.7 94.3 %all-gather.2.cloned.1.call-done = bf16[4096,768]{1,0:T(8,128)(2,1)} async-done(((bf16[128,768]{1,0:T(8,128)(2,1)}), bf16[4096,768]{1,0:T(8,128)(2,1)}) %all-gather.2.cloned.1.call-update) | async-done | bytes 6291472 | tf_op jit(solution)/shard_map/all_gather | solution.py:51
  120.1 9.0 %fusion.41 = f32[4096,384]{1,0:T(8,128)} fusion(bf16[4096,768]{1,0:T(8,128)(2,1)} %all-gather.2.cloned.1.call-done, bf16[768,384]{1,0:T(8,128)(2,1)} %param.11), kind=kOutput, calls=%fused_computation.70 | convolution fusion | flops 2415919104 | bytes 13172736 | tf_op jit(solution)/shard_map/dot_general | solution.py:50
  129.0 0.0 all-reduce.5.cloned.1.call-update
  129.1 0.0 reduce-scatter.2.cloned.1.call-start
  129.1 129.7 %all-reduce.5.cloned.1.call-done = f32[4096,384]{1,0:T(8,128)} async-done(((f32[4096,384]{1,0:T(8,128)}), f32[4096,384]{1,0:T(8,128)}) %all-reduce.5.cloned.1.call-update) | async-done | bytes 6291472 | tf_op jit(solution)/shard_map/psum | solution.py:55
  258.8 11.8 %fusion.8 = f32[4096,768]{1,0:T(8,128)} fusion(bf16[384,768]{1,0:T(8,128)(2,1)S(1)} %copy-done, f32[4096,384]{1,0:T(8,128)} %all-reduce.5.cloned.1.call-done), kind=kOutput, calls=%fused_computation.9 | convolution fusion | flops 2430074880 | bytes 19464192 | tf_op jit(solution)/shard_map/dot_general | solution.py:58
  270.6 0.0 reduce-scatter.2.cloned.1.call-update
  270.7 0.3 reduce-window.9
  271.0 0.1 slice.40
  271.7 0.1 slice_reduce_fusion
  271.8 0.1 multiply_bitcast_fusion
  271.9 0.7 select_reduce_fusion
  274.0 0.7 iota_compare_fusion.1
  274.7 1.3 compare_and_fusion
  275.9 167.3 %reduce-scatter.2.cloned.1.call-done = f32[128,768]{1,0:T(8,128)} async-done(((f32[4096,768]{1,0:T(8,128)}), f32[128,768]{1,0:T(8,128)}) %reduce-scatter.2.cloned.1.call-update) | async-done | bytes 393232 | tf_op jit(solution)/shard_map/reduce_scatter | solution.py:57
  443.2 1.3 convert_reduce_fusion
  444.5 0.0 copy-start.2
  444.5 10.5 %all-reduce.1 = (f32[128,1]{0,1:T(1,128)S(1)}, f32[128,1]{0,1:T(1,128)S(1)}) all-reduce(f32[128,1]{0,1:T(1,128)S(1)} %bitcast.50, f32[128,1]{0,1:T(1,128)S(1)} %bitcast.49), channel_id=1, replica_groups=mesh['cfg'=2,'wide'=32,'narrow'=4] {'narrow'}, use_global_device_ids=true, to_apply=%region_14.15 | all-reduce | flops 256 | bytes 2048 | tf_op jit(solution)/shard_map/psum | solution.py:23
  455.0 0.3 convolution_multiply_fusion
  455.3 31.1 %psum.47 = f32[128,64]{0,1:T(8,128)S(1)} all-reduce(f32[128,64]{0,1:T(8,128)S(1)} %convolution_multiply_fusion), channel_id=1, replica_groups=mesh['cfg'=2,'wide'=32,'narrow'=4] {'cfg','narrow'}, use_global_device_ids=true, to_apply=%region_15.16 | all-reduce | flops 8192 | bytes 65536 | tf_op jit(solution)/shard_map/psum | solution.py:68
  486.4 0.6 subtract_select_fusion
  (13 shorter events, 0.1 us)
Async XLA Ops:
  7.2 251.7 %copy-start = (bf16[384,768]{1,0:T(8,128)(2,1)S(1)}, bf16[384,768]{1,0:T(8,128)(2,1)}, u32[]{:S(2)}) copy-start(bf16[384,768]{1,0:T(8,128)(2,1)} %param.12) | copy-start | bytes 1769476
  7.2 112.9 %all-gather.2.cloned.1.call-start = ((), (), s32[]{:S(2)}) async-start(), calls=%async_computation.1 | async-start | bytes 6488064 | tf_op jit(solution)/shard_map/all_gather | solution.py:51
  25.7 233.1 %all-reduce.5.cloned.1.call-start = ((), (), s32[]{:S(2)}) async-start(), calls=%async_computation.2 | async-start | bytes 12582912 | tf_op jit(solution)/shard_map/psum | solution.py:55
  129.1 314.2 %reduce-scatter.2.cloned.1.call-start = ((), (), s32[]{:S(2)}) async-start(), calls=%async_computation.3 | async-start | bytes 12976128 | tf_op jit(solution)/shard_map/reduce_scatter | solution.py:57
  270.6 172.6 %copy-start.1 = (bf16[1,128,768]{2,1,0:T(8,128)(2,1)S(1)}, bf16[1,128,768]{2,1,0:T(8,128)(2,1)}, u32[]{:S(2)}) copy-start(bf16[1,128,768]{2,1,0:T(8,128)(2,1)} %param.8) | copy-start | bytes 589828
  270.6 184.4 %copy-start.4 = (bf16[768,64]{0,1:T(8,128)(2,1)S(1)}, bf16[768,64]{0,1:T(8,128)(2,1)}, u32[]{:S(2)}) copy-start(bf16[768,64]{0,1:T(8,128)(2,1)} %param.13) | copy-start | bytes 294916
  270.6 215.8 %copy-start.3 = (f32[128,64]{0,1:T(8,128)S(1)}, f32[128,64]{0,1:T(8,128)}, u32[]{:S(2)}) copy-start(f32[128,64]{0,1:T(8,128)} %param.14) | copy-start | bytes 98308
  444.5 42.6 %copy-start.2 = (bf16[128,768]{1,0:T(8,128)(2,1)}, bf16[128,768]{1,0:T(8,128)(2,1)S(1)}, u32[]{:S(2)}) copy-start(bf16[128,768]{1,0:T(8,128)(2,1)S(1)} %get-tuple-element.18) | copy-start | bytes 589828
Sparse Core Ops, SparseCore 0:
  25.8 94.2 all-gather.1
  129.2 129.5 all-reduce.4
  270.8 172.3 reduce-scatter.1
where the time goes:
time: 494 us
  waiting for transfers between devices  391 us (79%)
  blocking collectives  52.4 us (11%)
  matrix products  21.1 us (4%)
  between operations  15.9 us (3%)
  other arithmetic  12.5 us (3%)
    reduce_scatter x1, waiting for transfers between devices, on_device(): lax.psum_scatter(jnp.dot(activated, contract_weight, preferred_element_ty...  167 us
    psum x1, waiting for transfers between devices, on_device(): hidden_pre = lax.psum(hidden_part, 'narrow')  130 us
    all_gather x1, waiting for transfers between devices, on_device(): lax.all_gather(normed, 'wide', axis=0, tiled=True)  94.3 us
    psum x1, blocking collectives, on_device(): guided = lax.psum(velocity_part * copy_weight, ('cfg', 'narrow'))  31.1 us
    psum x2, blocking collectives, feature_norm(): lax.psum((jnp.sum(values, -1, keepdims=True), jnp.sum(values * values, -1...  21.2 us
    dot_general x1, matrix products, on_device(): jnp.dot(activated, contract_weight, preferred_element_type=jnp.float32)  11.8 us
  transfers between devices with their start and end apart: 3, of which 3 were waited for; matrix products, arithmetic and copies ran while one was open for 1% of the time, Pallas kernels for 0%

commit v1 on v0

v1 whole, which is shorter than its diff:
```python
import functools

import jax
import jax.numpy as jnp
import numpy as np
from jax import lax
from jax.experimental import pallas as pl
from jax.experimental.pallas import tpu as pltpu
from jax.sharding import PartitionSpec as P

TEXT = 226
EPS = 1e-05
GUIDANCE = 6.0
MESH = pl.DeviceIdType.MESH
F32 = jnp.float32
BF16 = jnp.bfloat16


def alpha_table():
    start_root = 0.00085**0.5
    end_root = 0.012**0.5
    roots = start_root + (end_root - start_root) * np.arange(1000) / 999.0
    table = np.zeros((8, 128), np.float32)
    table.reshape(-1)[:1000] = np.cumprod(1.0 - roots * roots)
    return table


def body(
    sizes,
    split_ref,
    time_ref,
    hidden_ref,
    mod_ref,
    w1_ref,
    w2_ref,
    ow_ref,
    latent_ref,
    alpha_ref,
    out_ref,
    clean_ref,
    xr,
    modg,
    owg,
    w1g,
    w2g,
    nst,
    xa,
    hid,
    act,
    sib_s,
    sib_r,
    ring_s,
    ring_r,
    tot,
    xs,
    xv,
    fs,
    fr,
    ffb,
    lo,
    vel_s,
    vel_r,
    cl,
    y_s,
    y_r,
    w_s,
    w_r,
    loc,
    ag_s,
    ag_r,
    sb_s,
    sb_r,
    x_s,
    x_r,
    i_s,
    i_r,
    pr_s,
    pr_r,
    rg_s,
    rg_r,
    c_s,
    c_r,
    o_s,
    o_r,
):
    nz, ny, q, bl, ff, feats = sizes
    half = 2 * q
    cfg = lax.axis_index("cfg")
    w = lax.axis_index("wide")
    n = lax.axis_index("narrow")
    core = lax.rem(w, 2)
    z = lax.rem(w // 2, nz)
    xh = w // (2 * nz)
    d = 1 - 2 * core

    def wide_of(xh_, z_, core_):
        return xh_ * (2 * nz) + z_ * 2 + core_

    def zmod(v):
        return lax.rem(v + 2 * nz, nz)

    def yid(k):
        return lax.rem(n + k, ny)

    sib = (cfg, wide_of(xh, z, 1 - core), n)
    xpart = (cfg, wide_of(1 - xh, z, core), n)
    znext = (cfg, wide_of(xh, zmod(z + d), core), n)
    zprev = (cfg, wide_of(xh, zmod(z - d), core), n)
    cpart = (1 - cfg, w, n)

    def ypeer(k):
        return (cfg, w, yid(k))

    def rcopy(src, dst, ssem, rsem, dev):
        return pltpu.make_async_remote_copy(
            src_ref=src, dst_ref=dst, send_sem=ssem, recv_sem=rsem, device_id=dev, device_id_type=MESH
        )

    def arrived(dst, rsem):
        rcopy(dst, dst, rsem, rsem, sib).wait_recv()

    def sent(src, ssem):
        rcopy(src, src, ssem, ssem, sib).wait_send()

    barrier = pltpu.get_barrier_semaphore()
    partners = [ypeer(1), ypeer(2), ypeer(3), sib, xpart, znext, zprev, cpart]
    for dev in partners:
        pl.semaphore_signal(barrier, inc=1, device_id=dev, device_id_type=MESH)
    pl.semaphore_wait(barrier, len(partners))

    def rows_of(i, size):
        return pl.ds(pl.multiple_of(i * size, size), size)

    for k in (1, 3, 2):
        m = yid(k)
        rcopy(hidden_ref.at[rows_of(m, q), :], xr.at[n], y_s.at[0, k - 1], y_r.at[0, k - 1], ypeer(k)).start()
    for k in (1, 3, 2):
        rcopy(mod_ref, modg.at[n], y_s.at[1, k - 1], y_r.at[1, k - 1], ypeer(k)).start()
    own = [
        (hidden_ref.at[rows_of(n, q), :], xr.at[n]),
        (mod_ref, modg.at[n]),
        (ow_ref, owg.at[n]),
        (w1_ref, w1g.at[n]),
        (w2_ref, w2g.at[n]),
    ]
    for i, (src, dst) in enumerate(own):
        pltpu.make_async_copy(src, dst, loc.at[i]).start()
    weights = [(w1_ref, w1g, bl // 2), (w2_ref, w2g, ff // 2)]

    def weight_out(i):
        src, dst, _ = weights[i]
        rcopy(src, dst.at[n], w_s.at[i, 0], w_r.at[i, 0], ypeer(1)).start()
        rcopy(src, dst.at[n], w_s.at[i, 1], w_r.at[i, 1], ypeer(3)).start()

    def weight_on(i):
        _, dst, part = weights[i]
        arrived(dst.at[yid(3)], w_r.at[i, 0])
        first = dst.at[yid(3), pl.ds(0, part), :]
        rcopy(first, first, w_s.at[i, 2], w_r.at[i, 2], ypeer(1)).start()
        arrived(dst.at[yid(1)], w_r.at[i, 1])
        second = dst.at[yid(1), pl.ds(part, part), :]
        rcopy(second, second, w_s.at[i, 3], w_r.at[i, 3], ypeer(3)).start()

    def weight_in(i):
        _, dst, part = weights[i]
        arrived(dst.at[yid(2), pl.ds(0, part), :], w_r.at[i, 2])
        arrived(dst.at[yid(2), pl.ds(part, part), :], w_r.at[i, 3])

    weight_out(0)
    for k in (1, 3, 2):
        rcopy(ow_ref, owg.at[n], y_s.at[2, k - 1], y_r.at[2, k - 1], ypeer(k)).start()

    offset = jnp.int32(0)
    count = jnp.int32(0)
    for b in range(split_ref.shape[0]):
        value = split_ref[b]
        offset = offset + jnp.where(b < w, value, 0)
        count = count + jnp.where(b == w, value, 0)
    slot = n * q + lax.broadcasted_iota(jnp.int32, (q, 1), 0)
    live = slot < count
    text = live & (slot + offset < TEXT)
    video = live & (slot + offset >= TEXT)

    def pick(b, row_text, row_video):
        return jnp.where(text, modg[b, pl.ds(row_text, 1), :], modg[b, pl.ds(row_video, 1), :])

    def stats(total, squares):
        average = total / feats
        variance = squares / feats - average * average
        return average, lax.rsqrt(variance + EPS)

    pltpu.make_async_copy(own[0][0], own[0][1], loc.at[0]).wait()
    pltpu.make_async_copy(own[1][0], own[1][1], loc.at[1]).wait()
    for k in (1, 2, 3):
        arrived(xr.at[yid(ny - k)], y_r.at[0, k - 1])
    total = jnp.zeros((q, 1), F32)
    squares = jnp.zeros((q, 1), F32)
    for b in range(ny):
        v = xr[b].astype(F32)
        total = total + jnp.sum(v, -1, keepdims=True)
        squares = squares + jnp.sum(v * v, -1, keepdims=True)
    average, scale = stats(total, squares)
    for k in (1, 2, 3):
        arrived(modg.at[yid(ny - k)], y_r.at[1, k - 1])
    for b in range(ny):
        v = xr[b].astype(F32)
        nst[b] = ((v - average) * scale * (1.0 + pick(b, 4, 1)) + pick(b, 3, 0)).astype(BF16)

    mine = 2 * core
    other = 2 * (1 - core)
    own_rows = rows_of(xh * 2 + core, q)
    sib_rows = rows_of(xh * 2 + 1 - core, q)
    a_rows = rows_of(xh, half)
    b_rows = rows_of(1 - xh, half)

    rcopy(
        nst.at[pl.ds(other, 2)], xa.at[z, pl.ds(other, 2), own_rows, :], i_s.at[0], i_r.at[0], sib
    ).start()
    for j in range(2):
        xa[z, mine + j, own_rows, :] = nst[mine + j]
    arrived(xa.at[z, pl.ds(mine, 2), sib_rows, :], i_r.at[0])

    def ag(o, rows):
        return xa.at[o, pl.ds(mine, 2), rows, :]

    def side(o, first):
        return xa.at[o, pl.ds(first, 2), :, :]

    rcopy(ag(z, a_rows), ag(z, a_rows), x_s.at[0], x_r.at[0], xpart).start()
    hid[...] = jnp.zeros_like(hid)

    def work(i, carry):
        o = zmod(z - d * i)
        hid[o] = hid[o] + (
            jnp.dot(xa[o, mine], w1g[mine], preferred_element_type=F32)
            + jnp.dot(xa[o, mine + 1], w1g[mine + 1], preferred_element_type=F32)
        )
        p = zmod(z + d * i)
        arrived(side(p, other), sb_r.at[i])
        hid[p] = hid[p] + (
            jnp.dot(xa[p, other], w1g[other], preferred_element_type=F32)
            + jnp.dot(xa[p, other + 1], w1g[other + 1], preferred_element_type=F32)
        )
        return carry

    def gelu(o):
        v = hid[o]
        act[o] = (0.5 * v * (1.0 + jnp.tanh(0.7978845608 * (v + 0.044715 * (v * v * v))))).astype(BF16)

    ready = min(3, nz - 2)
    done_work = 0
    for s in range(nz):
        o = zmod(z - d * s)
        last = s == nz - 1
        if s > 0:
            arrived(ag(o, a_rows), ag_r.at[s - 1, 0])
        if not last:
            rcopy(ag(o, a_rows), ag(o, a_rows), ag_s.at[s, 0], ag_r.at[s, 0], znext).start()
        if s == 0:
            arrived(ag(z, b_rows), x_r.at[0])
        else:
            arrived(ag(o, b_rows), ag_r.at[s - 1, 1])
        if not last:
            rcopy(ag(o, b_rows), ag(o, b_rows), ag_s.at[s, 1], ag_r.at[s, 1], znext).start()
        rcopy(side(o, mine), side(o, mine), sb_s.at[s], sb_r.at[s], sib).start()
        if s == min(2, nz - 2):
            pltpu.make_async_copy(own[3][0], own[3][1], loc.at[3]).wait()
            weight_on(0)
            weight_out(1)
        if s == ready:
            weight_in(0)
        if s >= ready:
            upto = nz if last else min(s, 2 * (s - ready) + 2)
            lax.fori_loop(done_work, upto, work, 0)
            done_work = upto
        if s == min(5, nz - 2):
            pltpu.make_async_copy(own[4][0], own[4][1], loc.at[4]).wait()
            weight_on(1)

    lax.fori_loop(0, nz, lambda i, carry: (gelu(i), carry)[1], 0)
    weight_in(1)

    def sib_part(s):
        p = zmod(z + d * (1 + s))
        for j in range(2):
            sib_s[s, j] = jnp.dot(act[p], w2g[other + j], preferred_element_type=F32).astype(BF16)
        rcopy(sib_s.at[s], sib_r.at[s], pr_s.at[s], pr_r.at[s], sib).start()

    def own_part(s, j):
        p = zmod(z - d * (1 + s))
        return jnp.dot(act[p], w2g[mine + j], preferred_element_type=F32)

    def ring_out(s, j):
        rcopy(ring_s.at[s, j], ring_r.at[s, j], rg_s.at[s, j], rg_r.at[s, j], znext).start()

    sib_part(0)
    sib_part(1)
    arrived(sib_r.at[0], pr_r.at[0])
    for j in range(2):
        ring_s[0, j] = (own_part(0, j) + sib_r[0, j].astype(F32)).astype(BF16)
        ring_out(0, j)

    def ring_step(s, carry):
        sib_part(s + 1)
        arrived(sib_r.at[s], pr_r.at[s])
        for j in range(2):
            part = own_part(s, j) + sib_r[s, j].astype(F32)
            arrived(ring_r.at[s - 1, j], rg_r.at[s - 1, j])
            ring_s[s, j] = (part + ring_r[s - 1, j].astype(F32)).astype(BF16)
            ring_out(s, j)
        return carry

    lax.fori_loop(1, nz - 1, ring_step, 0)
    end = nz - 1
    arrived(sib_r.at[end], pr_r.at[end])
    for j in range(2):
        tot[j] = own_part(end, j) + sib_r[end, j].astype(F32)
        arrived(ring_r.at[end - 1, j], rg_r.at[end - 1, j])
        tot[j] = tot[j] + ring_r[end - 1, j].astype(F32)
        xs[j] = tot[j, b_rows, :].astype(BF16)
        rcopy(xs.at[j], xv.at[j], x_s.at[1 + j], x_r.at[1 + j], xpart).start()
    for j in range(2):
        arrived(xv.at[j], x_r.at[1 + j])
        fs[j] = (tot[j, sib_rows, :] + xv[j, rows_of(1 - core, q), :].astype(F32)).astype(BF16)
    rcopy(fs, fr, i_s.at[1], i_r.at[1], sib).start()
    for j in range(2):
        ffb[mine + j] = tot[j, own_rows, :] + xv[j, rows_of(core, q), :].astype(F32)
    arrived(fr, i_r.at[1])
    for j in range(2):
        ffb[other + j] = fr[j].astype(F32)

    total = jnp.zeros((q, 1), F32)
    squares = jnp.zeros((q, 1), F32)
    for b in range(ny):
        v = xr[b].astype(F32) + pick(b, 5, 2) * ffb[b]
        v = jnp.where(live, v, 0.0).astype(BF16)
        lo[b] = v
        v = v.astype(F32)
        total = total + jnp.sum(v, -1, keepdims=True)
        squares = squares + jnp.sum(v * v, -1, keepdims=True)
    out_rows = rows_of(n, q)
    for k in (1, 3, 2):
        rcopy(lo.at[yid(k)], out_ref.at[out_rows, :], o_s.at[0, k - 1], o_r.at[0, k - 1], ypeer(k)).start()
    pltpu.make_async_copy(lo.at[n], out_ref.at[out_rows, :], loc.at[5]).start()
    average, scale = stats(total, squares)
    pltpu.make_async_copy(own[2][0], own[2][1], loc.at[2]).wait()
    for k in (1, 2, 3):
        arrived(owg.at[yid(ny - k)], y_r.at[2, k - 1])
    velocity = jnp.zeros((q, ow_ref.shape[1]), F32)
    for b in range(ny):
        v = (lo[b].astype(F32) - average) * scale
        v = (v * (1.0 + modg[b, pl.ds(7, 1), :]) + modg[b, pl.ds(6, 1), :]).astype(BF16)
        velocity = velocity + jnp.dot(v, owg[b], preferred_element_type=F32)
    vel_s[...] = velocity * jnp.where(cfg == 0, GUIDANCE, 1.0 - GUIDANCE)
    rcopy(vel_s, vel_r, c_s.at[0], c_r.at[0], cpart).start()
    index = lax.broadcasted_iota(jnp.int32, (8, 128), 0) * 128 + lax.broadcasted_iota(jnp.int32, (8, 128), 1)
    alpha = jnp.where(index == time_ref[0], alpha_ref[...], 0.0)
    alpha = jnp.sum(jnp.sum(alpha, 0, keepdims=True), 1, keepdims=True)
    scaled = jnp.sqrt(alpha) * latent_ref[out_rows, :]
    arrived(vel_r, c_r.at[0])
    guided = vel_s[...] + vel_r[...]
    cl[...] = jnp.where(video, scaled - jnp.sqrt(1.0 - alpha) * guided, 0.0)
    for k in (1, 3, 2):
        rcopy(cl, clean_ref.at[out_rows, :], o_s.at[1, k - 1], o_r.at[1, k - 1], ypeer(k)).start()
    pltpu.make_async_copy(cl, clean_ref.at[out_rows, :], loc.at[6]).start()

    for k in (1, 2, 3):
        sent(hidden_ref.at[rows_of(yid(k), q), :], y_s.at[0, k - 1])
        sent(mod_ref, y_s.at[1, k - 1])
        sent(ow_ref, y_s.at[2, k - 1])
    for i, (src, dst, part) in enumerate(weights):
        sent(src, w_s.at[i, 0])
        sent(src, w_s.at[i, 1])
        sent(dst.at[yid(3), pl.ds(0, part), :], w_s.at[i, 2])
        sent(dst.at[yid(1), pl.ds(part, part), :], w_s.at[i, 3])
    sent(nst.at[pl.ds(other, 2)], i_s.at[0])
    sent(ag(z, a_rows), x_s.at[0])
    for s in range(nz):
        o = zmod(z - d * s)
        if s < nz - 1:
            sent(ag(o, a_rows), ag_s.at[s, 0])
            sent(ag(o, b_rows), ag_s.at[s, 1])
            for j in range(2):
                sent(ring_s.at[s, j], rg_s.at[s, j])
        sent(side(o, mine), sb_s.at[s])
        sent(sib_s.at[s], pr_s.at[s])
    for j in range(2):
        sent(xs.at[j], x_s.at[1 + j])
    sent(fs, i_s.at[1])
    sent(vel_s, c_s.at[0])
    for k in (1, 2, 3):
        sent(lo.at[yid(k)], o_s.at[0, k - 1])
        sent(cl, o_s.at[1, k - 1])
        arrived(out_ref.at[rows_of(yid(ny - k), q), :], o_r.at[0, k - 1])
        arrived(clean_ref.at[rows_of(yid(ny - k), q), :], o_r.at[1, k - 1])
    pltpu.make_async_copy(lo.at[n], out_ref.at[out_rows, :], loc.at[5]).wait()
    pltpu.make_async_copy(cl, clean_ref.at[out_rows, :], loc.at[6]).wait()


def on_device(n_wide, n_narrow, hidden, split_table, modulation, w1, w2, ow, latent, timestep):
    cap, bl = hidden.shape[1:]
    ff = w1.shape[1]
    patch = ow.shape[1]
    ny = n_narrow
    nz = n_wide // 4
    q = cap // ny
    rows = 4 * q
    sizes = (nz, ny, q, bl, ff, bl * ny)
    dma = pltpu.SemaphoreType.DMA
    vm = pltpu.VMEM
    scratch = [
        vm((ny, q, bl), BF16),
        vm((ny, 8, bl), F32),
        vm((ny, bl, patch), BF16),
        vm((ny, bl, ff), BF16),
        vm((ny, ff, bl), BF16),
        vm((ny, q, bl), BF16),
        vm((nz, ny, rows, bl), BF16),
        vm((nz, rows, ff), F32),
        vm((nz, rows, ff), BF16),
        vm((nz, 2, rows, bl), BF16),
        vm((nz, 2, rows, bl), BF16),
        vm((nz - 1, 2, rows, bl), BF16),
        vm((nz - 1, 2, rows, bl), BF16),
        vm((2, rows, bl), F32),
        vm((2, 2 * q, bl), BF16),
        vm((2, 2 * q, bl), BF16),
        vm((2, q, bl), BF16),
        vm((2, q, bl), BF16),
        vm((ny, q, bl), F32),
        vm((ny, q, bl), BF16),
        vm((q, patch), F32),
        vm((q, patch), F32),
        vm((q, patch), F32),
        dma((3, 3)),
        dma((3, 3)),
        dma((2, 4)),
        dma((2, 4)),
        dma((7,)),
        dma((nz - 1, 2)),
        dma((nz - 1, 2)),
        dma((nz,)),
        dma((nz,)),
        dma((3,)),
        dma((3,)),
        dma((2,)),
        dma((2,)),
        dma((nz,)),
        dma((nz,)),
        dma((nz - 1, 2)),
        dma((nz - 1, 2)),
        dma((1,)),
        dma((1,)),
        dma((2, 3)),
        dma((2, 3)),
    ]
    anyspec = pl.BlockSpec(memory_space=pl.ANY)
    smem = pl.BlockSpec(memory_space=pltpu.SMEM)
    vmem = pl.BlockSpec(memory_space=pltpu.VMEM)
    layer_out, clean = pl.pallas_call(
        functools.partial(body, sizes),
        out_shape=(
            jax.ShapeDtypeStruct((cap, bl), BF16),
            jax.ShapeDtypeStruct((cap, patch), F32),
        ),
        in_specs=[smem, smem, anyspec, anyspec, anyspec, anyspec, anyspec, vmem, vmem],
        out_specs=(anyspec, anyspec),
        scratch_shapes=scratch,
        compiler_params=pltpu.CompilerParams(
            collective_id=0, has_side_effects=True, vmem_limit_bytes=48 * 1024 * 1024
        ),
    )(
        split_table,
        timestep,
        hidden[0],
        modulation,
        w1,
        w2,
        ow,
        latent,
        jnp.asarray(alpha_table()),
    )
    return (layer_out[None], clean)


def solution(mesh):
    return jax.shard_map(
        functools.partial(on_device, mesh.shape["wide"], mesh.shape["narrow"]),
        mesh=mesh,
        in_specs=(
            P("cfg", "wide", "narrow"),
            P(),
            P(None, "narrow"),
            P("narrow", "wide"),
            P("wide", "narrow"),
            P("narrow", None),
            P("wide", None),
            P(),
        ),
        out_specs=(P("cfg", "wide", "narrow"), P("wide", None)),
        check_vma=False,
    )
```

time: 494 us -> 122 us (0.25)
  waiting for transfers between devices: 391 us -> 0 us
  Pallas kernels: 0 us -> 114 us
  blocking collectives: 52.4 us -> 0 us
  matrix products: 21.1 us -> 0 us
  between operations: 15.9 us -> 1.39 us
  other arithmetic: 12.5 us -> 0 us
    reduce_scatter x1 -> x0, waiting for transfers between devices: 167 us -> none  [on_device(): lax.psum_scatter(jnp.dot(activated, contract_weight, preferred_element_ty...]
    psum x1 -> x0, waiting for transfers between devices: 130 us -> none  [on_device(): hidden_pre = lax.psum(hidden_part, 'narrow')]
    pallas_call x0 -> x1, Pallas kernels: none -> 114 us  [on_device(): pl.pallas_call(functools.partial(body, sizes), out_shape=(jax.ShapeDtypeS...]
    all_gather x1 -> x0, waiting for transfers between devices: 94.3 us -> none  [on_device(): lax.all_gather(normed, 'wide', axis=0, tiled=True)]
    psum x3 -> x0, blocking collectives: 52.4 us -> none  [the longest x1 31.1 us: on_device(): guided = lax.psum(velocity_part * copy_weight, ('cfg', 'narrow'))]
    dot_general x3 -> x0, matrix products: 21.1 us -> none  [the longest x1 11.8 us: on_device(): jnp.dot(activated, contract_weight, preferred_element_type=jnp.float32)]
    reduce_sum x5 -> x0, other arithmetic: 5.4 us -> none  [the longest x2 2.34 us: feature_norm(): jnp.sum(values, -1, keepdims=True)]
    unnamed x10 -> x18, local copies, waits for them, and re-layouts: 0.03 us -> 5.12 us
  transfers between devices with their start and end apart: 3 -> 0, of which waited for: 3 -> 0; matrix products, arithmetic and copies ran while one was open for 1% -> 0% of each run, Pallas kernels for 0% -> 0%
where the time goes in v1:
time: 122 us; the launch traced here: 121 us
  Pallas kernels  114 us (93%)
  local copies, waits for them, and re-layouts  5.12 us (4%)
  between operations  1.39 us (1%)
    pallas_call x1, Pallas kernels, on_device(): pl.pallas_call(functools.partial(body, sizes), out_shape=(jax.ShapeDtypeS...  114 us
    unnamed x18, local copies, waits for them, and re-layouts  5.12 us

profile of v1, /device:TPU:2, one launch (start us, length us, event | category | flops | bytes accessed | tf_op | source)
XLA Modules:
  0.0 120.8 jit_solution(1664502034258862573)
XLA Ops:
  0.6 0.0 copy-start.6
  1.3 0.0 copy-start.2
  1.3 0.9 copy.12.latent_ref
  2.2 0.0 copy-done.6
  2.2 0.0 copy-start.3
  2.2 0.0 copy-start.4
  2.3 0.0 copy-start.5
  2.3 0.2 copy.11.ow_ref
  2.4 0.0 copy-done.2
  2.4 0.5 copy-done.3
  3.0 0.0 copy-done.4
  3.0 0.0 copy-done.5
  3.0 0.0 copy-start
  3.0 1.1 copy-done
  4.1 0.0 copy-start.1
  4.1 1.1 copy-done.1
  5.1 114.3 %shard_map.104 = (bf16[128,768]{1,0:T(8,128)(2,1)S(1)}, f32[128,64]{1,0:T(8,128)S(1)}) custom-call(s32[32]{0:T(128)S(1)} %copy-done.5, s32[1]{0:T(128)S(6)} %copy.15.time_ref, bf16[128,768]{1,0:T(8,128)(2,1)S(1)} %bitcast.3, f32[8,768]{1,0:T(8,128)S(1)} %copy-done.3, bf16[768,384]{1,0:T(8,128)(2,1)S(1)} %copy-done, bf16[384,768]{1,0:T(8,128)(2,1)S(1)} %copy-done.1, ...), custom_call_target="tpu_custom_call" | custom-call | tf_op jit(solution)/shard_map/pallas_call | solution.py:460
  119.4 0.7 copy.13
  120.1 0.7 copy.16
Async XLA Ops:
  0.6 1.6 %copy-start.6 = (bf16[768,64]{0,1:T(8,128)(2,1)S(1)}, bf16[768,64]{0,1:T(8,128)(2,1)}, u32[]{:S(2)}) copy-start(bf16[768,64]{0,1:T(8,128)(2,1)} %param.14) | copy-start | bytes 294916
  1.3 1.1 copy-start.2
  2.2 0.7 copy-start.3
  2.2 0.7 copy-start.4
  2.3 0.7 copy-start.5
  3.0 1.1 copy-start
  4.1 1.1 copy-start.1

commit v2 on v1

v2 whole, which is shorter than its diff:
```python
import functools

import jax
import jax.numpy as jnp
import numpy as np
from jax import lax
from jax.experimental import pallas as pl
from jax.experimental.pallas import tpu as pltpu
from jax.sharding import PartitionSpec as P

TEXT = 226
EPS = 1e-05
GUIDANCE = 6.0
MESH = pl.DeviceIdType.MESH
F32 = jnp.float32
BF16 = jnp.bfloat16
I32 = jnp.int32


def alpha_table():
    start_root = 0.00085**0.5
    end_root = 0.012**0.5
    roots = start_root + (end_root - start_root) * np.arange(1000) / 999.0
    table = np.zeros((8, 128), np.float32)
    table.reshape(-1)[:1000] = np.cumprod(1.0 - roots * roots)
    return table


def dot(a, b):
    return jnp.dot(a, b, preferred_element_type=F32)


def dot_nt(a, b):
    return lax.dot_general(a, b, (((1,), (1,)), ((), ())), preferred_element_type=F32)


def iota(shape, dim):
    return lax.broadcasted_iota(I32, shape, dim)


def one_hot(condition):
    return jnp.where(condition, 1.0, 0.0).astype(BF16)


def body(
    sizes,
    split_ref,
    time_ref,
    hidden_ref,
    latent_ref,
    alpha_ref,
    mod_ref,
    w1_ref,
    w2_ref,
    ow_ref,
    out_ref,
    clean_ref,
    slab_s,
    slab_r,
    xr,
    modg,
    owg,
    w1g,
    w2g,
    nst,
    gx,
    spread,
    xa,
    hid,
    act,
    sib_s,
    sib_r,
    ring_s,
    ring_r,
    tot,
    es,
    er,
    ffb,
    lo,
    back_s,
    back_r,
    vel_s,
    vel_r,
    a_s,
    a_r,
    b_s,
    b_r,
    y_s,
    y_r,
    w_s,
    w_r,
    loc,
    e_s,
    e_r,
    ag_s,
    ag_r,
    sb_s,
    sb_r,
    pr_s,
    pr_r,
    rg_s,
    rg_r,
    f_s,
    f_r,
    c_s,
    c_r,
):
    nz, ny, q, gr, bl, ff, cap, patch = sizes
    feats = ny * bl
    hb = bl // 2
    groups = ny * nz
    la, lb = nz // 2, nz - 1 - nz // 2
    cfg = lax.axis_index("cfg")
    w = lax.axis_index("wide")
    n = lax.axis_index("narrow")
    core = lax.rem(w, 2)
    z = lax.rem(w // 2, nz)
    xh = w // (2 * nz)
    d = 1 - 2 * core

    def wide_of(xh_, z_, core_):
        return xh_ * (2 * nz) + z_ * 2 + core_

    def zmod(v):
        return lax.rem(v + 2 * nz, nz)

    def yid(k):
        return lax.rem(n + k, ny)

    sib = (cfg, wide_of(xh, z, 1 - core), n)
    xpart = (cfg, wide_of(1 - xh, z, core), n)
    diag = (cfg, wide_of(1 - xh, z, 1 - core), n)
    znext = (cfg, wide_of(xh, zmod(z + d), core), n)
    zprev = (cfg, wide_of(xh, zmod(z - d), core), n)
    cpart = (1 - cfg, w, n)

    def ypeer(k):
        return (cfg, w, yid(k))

    def peer(k):
        m = lax.rem(n + k // nz, ny)
        zd = lax.rem(z + lax.rem(k, nz), nz)
        return m * nz + zd, (cfg, wide_of(xh, zd, core), m)

    def source(k):
        m = lax.rem(n + ny - k // nz, ny)
        zd = lax.rem(z + nz - lax.rem(k, nz), nz)
        return m * nz + zd

    def rcopy(src, dst, ssem, rsem, dev):
        return pltpu.make_async_remote_copy(
            src_ref=src, dst_ref=dst, send_sem=ssem, recv_sem=rsem, device_id=dev, device_id_type=MESH
        )

    def arrived(dst, rsem):
        rcopy(dst, dst, rsem, rsem, sib).wait_recv()

    def sent(src, ssem):
        rcopy(src, src, ssem, ssem, sib).wait_send()

    def signal(dev):
        pl.semaphore_signal(barrier, inc=1, device_id=dev, device_id_type=MESH)

    def times(count, action, first=0):
        def step(k, carry):
            action(k)
            return carry

        lax.fori_loop(first, count, step, 0)

    barrier = pltpu.get_barrier_semaphore()
    times(groups, lambda k: signal(peer(k)[1]), 1)
    for dev in (sib, xpart, diag, cpart):
        signal(dev)

    own = [(mod_ref, modg.at[n]), (w1_ref, w1g.at[n]), (w2_ref, w2g.at[n]), (ow_ref, owg.at[n])]
    for i, (src, dst) in enumerate(own):
        pltpu.make_async_copy(src, dst, loc.at[i]).start()

    def rows_of(i, size):
        return pl.ds(pl.multiple_of(i * size, size), size)

    offset = jnp.int32(0)
    count = jnp.int32(0)
    for b in range(split_ref.shape[0]):
        value = split_ref[b]
        offset = offset + jnp.where(b < w, value, 0)
        count = count + jnp.where(b == w, value, 0)
    row = iota((groups * 8, cap), 0)
    residue = (row >> 3) * 4 + (row & 3)
    hit = residue == ((iota((groups * 8, cap), 1) + offset) & (cap - 1))
    low = (row & 4) == 0
    slabs = dot(one_hot(hit & low), hidden_ref[:, :hb]) + dot(one_hot(hit & ~low), hidden_ref[:, hb:])
    slab_s[...] = slabs.reshape(groups, 8, hb).astype(BF16)
    pl.semaphore_wait(barrier, groups - 1 + 4)

    def slab_out(k):
        target, dev = peer(k)
        rcopy(slab_s.at[target], slab_r.at[n * nz + z], a_s.at[k - 1], a_r.at[k - 1], dev).start()

    times(groups, slab_out, 1)
    for k in (1, 3, 2):
        rcopy(mod_ref, modg.at[n], y_s.at[0, k - 1], y_r.at[0, k - 1], ypeer(k)).start()
    slab_r[n * nz + z] = slab_s[n * nz + z]
    weights = [(w1_ref, w1g, bl // 2), (w2_ref, w2g, ff // 2)]

    def weight_out(i):
        src, dst, _ = weights[i]
        rcopy(src, dst.at[n], w_s.at[i, 0], w_r.at[i, 0], ypeer(1)).start()
        rcopy(src, dst.at[n], w_s.at[i, 1], w_r.at[i, 1], ypeer(3)).start()

    def weight_on(i):
        _, dst, part = weights[i]
        pltpu.make_async_copy(own[1 + i][0], own[1 + i][1], loc.at[1 + i]).wait()
        arrived(dst.at[yid(3)], w_r.at[i, 0])
        first = dst.at[yid(3), pl.ds(0, part), :]
        rcopy(first, first, w_s.at[i, 2], w_r.at[i, 2], ypeer(1)).start()
        arrived(dst.at[yid(1)], w_r.at[i, 1])
        second = dst.at[yid(1), pl.ds(part, part), :]
        rcopy(second, second, w_s.at[i, 3], w_r.at[i, 3], ypeer(3)).start()

    def weight_in(i):
        _, dst, part = weights[i]
        arrived(dst.at[yid(2), pl.ds(0, part), :], w_r.at[i, 2])
        arrived(dst.at[yid(2), pl.ds(part, part), :], w_r.at[i, 3])

    weight_out(0)
    for k in (1, 3, 2):
        rcopy(ow_ref, owg.at[n], y_s.at[1, k - 1], y_r.at[1, k - 1], ypeer(k)).start()
    hid[...] = jnp.zeros_like(hid)

    def slot_table(shape, dim):
        index = iota(shape, dim)
        member = index // q
        inner = index - member * q
        block = (member >> 1) * (2 * nz) + (inner >> 2) * 2 + (member & 1)
        off = jnp.zeros(shape, I32)
        cnt = jnp.zeros(shape, I32)
        for b in range(split_ref.shape[0]):
            value = split_ref[b]
            off = off + jnp.where(block > b, value, 0)
            cnt = cnt + jnp.where(block == b, value, 0)
        lane = inner & 3
        inside = ((n * nz + z) * 4 + lane - off) & (cap - 1)
        position = off + inside
        live = inside < cnt
        spot = jnp.where(live, lane * (gr // 4) + position // cap, -1)
        return live, position, spot

    lane_spot = slot_table((1, 4 * q), 1)[2]
    compact = one_hot(iota((gr, 4 * q), 0) == lane_spot)
    row_live, row_position, row_spot = slot_table((4 * q, 1), 0)
    spread[...] = jnp.where(iota((4 * q, gr), 1) == row_spot, 1.0, 0.0)
    member = xh * 2 + core
    state = jnp.where(row_live, jnp.where(row_position < TEXT, 2, 1), 0)
    tables = jnp.zeros((q, 1), I32)
    for i in range(4):
        tables = tables + jnp.where(member == i, state[i * q : (i + 1) * q], 0)
    live = tables > 0
    text = tables == 2

    def pick(b, row_text, row_video):
        return jnp.where(text, modg[b, pl.ds(row_text, 1), :], modg[b, pl.ds(row_video, 1), :])

    def stats(total, squares):
        average = total / feats
        variance = squares / feats - average * average
        return average, lax.rsqrt(variance + EPS)

    unrow = iota((q, 2 * q), 0)
    uncol = iota((q, 2 * q), 1)
    unhit = ((unrow >> 2) == (uncol >> 3)) & ((unrow & 3) == (uncol & 3))
    unlow = (uncol & 4) == 0
    take_low = one_hot(unhit & unlow)
    take_high = one_hot(unhit & ~unlow)
    times(groups, lambda k: arrived(slab_r.at[source(k)], a_r.at[k - 1]), 1)
    total = jnp.zeros((q, 1), F32)
    squares = jnp.zeros((q, 1), F32)
    for b in range(ny):
        v = slab_r[b * nz : (b + 1) * nz].astype(F32).reshape(nz * 8, hb).astype(BF16)
        for part, take in ((0, take_low), (1, take_high)):
            u = dot(take, v)
            xr[b, :, part * hb : (part + 1) * hb] = u.astype(BF16)
            total = total + jnp.sum(u, -1, keepdims=True)
            squares = squares + jnp.sum(u * u, -1, keepdims=True)
    average, scale = stats(total, squares)
    pltpu.make_async_copy(own[0][0], own[0][1], loc.at[0]).wait()
    for k in (1, 2, 3):
        arrived(modg.at[yid(ny - k)], y_r.at[0, k - 1])
    for b in range(ny):
        v = xr[b].astype(F32)
        nst[b] = ((v - average) * scale * (1.0 + pick(b, 4, 1)) + pick(b, 3, 0)).astype(BF16)

    mine = 2 * core
    other = 2 * (1 - core)
    own_rows = rows_of(member, q)
    mates = [(sib, xh * 2 + 1 - core, other), (xpart, (1 - xh) * 2 + core, mine), (diag, (1 - xh) * 2 + 1 - core, other)]
    for i in (1, 2, 0):
        dev, _, blk = mates[i]
        rcopy(nst.at[pl.ds(blk, 2)], gx.at[:, own_rows, :], e_s.at[i], e_r.at[i], dev).start()
    for j in range(2):
        gx[j, own_rows, :] = nst[mine + j]
    for i in range(3):
        arrived(gx.at[:, rows_of(mates[i][1], q), :], e_r.at[i])
    for j in range(2):
        xa[z, mine + j] = dot(compact, gx[j]).astype(BF16)

    def side(o, first):
        return xa.at[o, pl.ds(first, 2)]

    def relay(o, j, sem, dev):
        rcopy(xa.at[o, mine + j], xa.at[o, mine + j], ag_s.at[sem, j], ag_r.at[sem, j], dev).start()

    def share(u):
        o = zmod(z + d * u)
        rcopy(side(o, mine), side(o, mine), sb_s.at[u % nz], sb_r.at[u % nz], sib).start()

    def work(u):
        o = zmod(z + d * u)
        hid[o] = hid[o] + (dot(xa[o, mine], w1g[mine]) + dot(xa[o, mine + 1], w1g[mine + 1]))
        p = zmod(z - d * u)
        arrived(side(p, other), sb_r.at[zmod(u)])
        hid[p] = hid[p] + (dot(xa[p, other], w1g[other]) + dot(xa[p, other + 1], w1g[other + 1]))

    def gelu(o):
        v = hid[o]
        act[o] = (0.5 * v * (1.0 + jnp.tanh(0.7978845608 * (v + 0.044715 * (v * v * v))))).astype(BF16)

    for s in range(la):
        for j in range(2):
            if s > 0:
                arrived(xa.at[zmod(z - d * s), mine + j], ag_r.at[s - 1, j])
            relay(zmod(z - d * s), j, s, znext)
            if 0 < s <= lb:
                arrived(xa.at[zmod(z + d * s), mine + j], ag_r.at[la + s - 1, j])
            if s < lb:
                relay(zmod(z + d * s), j, la + s, zprev)
        share(-s)
        if 0 < s <= lb:
            share(s)
        if s == min(1, la - 1):
            weight_on(0)
            weight_out(1)
        if s == la - 1:
            weight_in(0)
            work(0)

            def pair(k):
                work(k)
                work(-k)

            times(la, pair, 1)
    for j in range(2):
        arrived(xa.at[zmod(z - d * la), mine + j], ag_r.at[la - 1, j])
    share(-la)
    for s in range(la, lb + 1):
        for j in range(2):
            arrived(xa.at[zmod(z + d * s), mine + j], ag_r.at[la + s - 1, j])
        share(s)
    weight_on(1)
    for u in range(la, nz - la + 1):
        work(u)
    times(nz, gelu)

    far = lax.rem(n + 2, ny)

    def blk_of(side_, b):
        near = side_ == n // 2
        first = jnp.where(near, n, far + 1 - 2 * lax.rem(far, 2))
        second = jnp.where(near, n + 1 - 2 * lax.rem(n, 2), far)
        return first if b == 0 else second

    order = []
    for s in range(la):
        order.append(("next", s, la - s))
        if s < lb:
            order.append(("prev", s, -(lb - s)))
    order.append(("stay", 0, 0))
    slot_of = {(kind, s): t for t, (kind, s, _) in enumerate(order)}

    def sib_part(t, b):
        p = zmod(z - d * order[t][2])
        sib_s[t, b] = dot(act[p], w2g[blk_of(1 - core, b)]).astype(BF16)
        rcopy(sib_s.at[t, b], sib_r.at[t, b], pr_s.at[t, b], pr_r.at[t, b], sib).start()

    def ring_part(t, b):
        kind, s, u = order[t]
        part = dot(act[zmod(z + d * u)], w2g[blk_of(core, b)])
        arrived(sib_r.at[t, b], pr_r.at[t, b])
        part = part + sib_r[t, b].astype(F32)
        if kind == "stay":
            before = [slot_of[("next", la - 1)]] + ([slot_of[("prev", lb - 1)]] if lb else [])
        else:
            before = [slot_of[(kind, s - 1)]] if s else []
        for p in before:
            arrived(ring_r.at[p, b], rg_r.at[p, b])
            part = part + ring_r[p, b].astype(F32)
        if kind == "stay":
            tot[b] = part.astype(BF16)
            for i in range(3):
                dev, index, _ = mates[i]
                es[i, b] = dot(spread[rows_of(index, q), :].astype(BF16), tot[b]).astype(BF16)
                rcopy(es.at[i, b], er.at[i, b], f_s.at[i, b], f_r.at[i, b], dev).start()
            return
        ring_s[t, b] = part.astype(BF16)
        rcopy(
            ring_s.at[t, b], ring_r.at[t, b], rg_s.at[t, b], rg_r.at[t, b], znext if kind == "next" else zprev
        ).start()

    stages = {}
    for t, (kind, s, _) in enumerate(order):
        stages.setdefault(la if kind == "stay" else s, []).append(t)
    lag = 2
    events = []
    for step in range(la + 1 + lag):
        for b in range(2):
            at = step - lag * b
            if 0 <= at <= la:
                events += [(t, b) for t in stages[at]]
    ahead = 2
    for t, b in events[:ahead]:
        sib_part(t, b)
    needs_far = False
    for i, (t, b) in enumerate(events):
        if i + ahead < len(events):
            if events[i + ahead][1] == 1 and not needs_far:
                weight_in(1)
                needs_far = True
            sib_part(*events[i + ahead])
        ring_part(t, b)

    for b in range(2):
        arrived(er.at[1, b], f_r.at[1, b])
        ffb[blk_of(core, b)] = dot(spread[own_rows, :].astype(BF16), tot[b]) + er[1, b].astype(F32)
    for b in range(2):
        arrived(er.at[0, b], f_r.at[0, b])
        arrived(er.at[2, b], f_r.at[2, b])
        ffb[blk_of(1 - core, b)] = er[0, b].astype(F32) + er[2, b].astype(F32)
    total = jnp.zeros((q, 1), F32)
    squares = jnp.zeros((q, 1), F32)
    for b in range(ny):
        v = xr[b].astype(F32) + pick(b, 5, 2) * ffb[b]
        v = jnp.where(live, v, 0.0).astype(BF16)
        lo[b] = v
        v = v.astype(F32)
        total = total + jnp.sum(v, -1, keepdims=True)
        squares = squares + jnp.sum(v * v, -1, keepdims=True)
    average, scale = stats(total, squares)
    pltpu.make_async_copy(own[3][0], own[3][1], loc.at[3]).wait()
    for k in (1, 2, 3):
        arrived(owg.at[yid(ny - k)], y_r.at[1, k - 1])
    velocity = jnp.zeros((q, patch), F32)
    for b in range(ny):
        v = (lo[b].astype(F32) - average) * scale
        v = (v * (1.0 + modg[b, pl.ds(7, 1), :]) + modg[b, pl.ds(6, 1), :]).astype(BF16)
        velocity = velocity + dot_nt(v, owg[b])
    velocity = velocity * jnp.where(cfg == 0, GUIDANCE, 1.0 - GUIDANCE)

    coarse = velocity.astype(BF16)
    fine = (velocity - coarse.astype(F32)).astype(BF16)
    backrow = iota((2 * q, q), 0)
    backcol = iota((2 * q, q), 1)
    backhit = ((backcol >> 2) == (backrow >> 3)) & ((backcol & 3) == (backrow & 3))
    backlow = (backrow & 4) == 0
    put_low = one_hot(backhit & backlow)
    put_high = one_hot(backhit & ~backlow)
    terms = dot(put_low, jnp.concatenate([coarse, fine], axis=1)).reshape(nz, 8, 2 * patch).astype(BF16)
    for b in range(ny):
        v = dot(put_low, lo[b, :, :hb]) + dot(put_high, lo[b, :, hb:])
        back_s[b * nz : (b + 1) * nz, :, :hb] = v.reshape(nz, 8, hb).astype(BF16)
        back_s[b * nz : (b + 1) * nz, :, hb:] = terms

    def back_out(k):
        target, dev = peer(k)
        rcopy(back_s.at[target], back_r.at[n * nz + z], b_s.at[k - 1], b_r.at[k - 1], dev).start()

    times(groups, back_out, 1)
    back_r[n * nz + z] = back_s[n * nz + z]

    column = iota((cap, groups * 8), 1)
    undo = ((column >> 3) * 4 + (column & 3)) == ((iota((cap, groups * 8), 0) + offset) & (cap - 1))
    undo_low = one_hot(undo & ((column & 4) == 0))
    undo_high = one_hot(undo & ((column & 4) != 0))
    index = iota((8, 128), 0) * 128 + iota((8, 128), 1)
    alpha = jnp.where(index == time_ref[0], alpha_ref[...], 0.0)
    alpha = jnp.sum(jnp.sum(alpha, 0, keepdims=True), 1, keepdims=True)
    scaled = jnp.sqrt(alpha) * latent_ref[...]
    factor = jnp.sqrt(1.0 - alpha)
    lanes = iota((1, cap), 1)
    video = (lanes < count) & (lanes + offset >= TEXT)
    times(groups, lambda k: arrived(back_r.at[source(k)], b_r.at[k - 1]), 1)
    v = back_r[:, :, hb:].astype(F32).reshape(groups * 8, 2 * patch).astype(BF16)
    v = dot(undo_low, v).T
    vel_s[...] = v[:patch] + v[patch:]
    rcopy(vel_s, vel_r, c_s.at[0], c_r.at[0], cpart).start()
    v = back_r[:, :, :hb].astype(F32).reshape(groups * 8, hb).astype(BF16)
    out_ref[:, :hb] = dot(undo_low, v).astype(BF16)
    out_ref[:, hb:] = dot(undo_high, v).astype(BF16)

    def slabs_sent(k):
        target = peer(k)[0]
        sent(slab_s.at[target], a_s.at[k - 1])
        sent(back_s.at[target], b_s.at[k - 1])

    times(groups, slabs_sent, 1)
    for k in (1, 2, 3):
        sent(mod_ref, y_s.at[0, k - 1])
        sent(ow_ref, y_s.at[1, k - 1])
    for i, (src, dst, part) in enumerate(weights):
        sent(src, w_s.at[i, 0])
        sent(src, w_s.at[i, 1])
        sent(dst.at[yid(3), pl.ds(0, part), :], w_s.at[i, 2])
        sent(dst.at[yid(1), pl.ds(part, part), :], w_s.at[i, 3])
    for i in range(3):
        sent(nst.at[pl.ds(mates[i][2], 2)], e_s.at[i])
        for b in range(2):
            sent(es.at[i, b], f_s.at[i, b])
    for s in range(la):
        for j in range(2):
            sent(xa.at[zmod(z - d * s), mine + j], ag_s.at[s, j])
    for s in range(lb):
        for j in range(2):
            sent(xa.at[zmod(z + d * s), mine + j], ag_s.at[la + s, j])
    for t in range(nz):
        sent(side(zmod(z + d * t), mine), sb_s.at[t])
        for b in range(2):
            sent(sib_s.at[t, b], pr_s.at[t, b])
            if t < nz - 1:
                sent(ring_s.at[t, b], rg_s.at[t, b])
    arrived(vel_r, c_r.at[0])
    clean_ref[...] = jnp.where(video, scaled - factor * (vel_s[...] + vel_r[...]), 0.0)
    sent(vel_s, c_s.at[0])


def on_device(n_wide, n_narrow, hidden, split_table, modulation, w1, w2, ow, latent, timestep):
    cap, bl = hidden.shape[1:]
    ff = w1.shape[1]
    patch = ow.shape[1]
    ny = n_narrow
    nz = n_wide // 4
    q = cap // ny
    gr = n_wide * 2
    sizes = (nz, ny, q, gr, bl, ff, cap, patch)
    groups = ny * nz
    hb = bl // 2
    dma = pltpu.SemaphoreType.DMA
    vm = pltpu.VMEM
    scratch = [
        vm((groups, 8, hb), BF16),
        vm((groups, 8, hb), BF16),
        vm((ny, q, bl), BF16),
        vm((ny, 8, bl), F32),
        vm((ny, patch, bl), BF16),
        vm((ny, bl, ff), BF16),
        vm((ny, ff, bl), BF16),
        vm((ny, q, bl), BF16),
        vm((2, 4 * q, bl), BF16),
        vm((4 * q, gr), F32),
        vm((nz, ny, gr, bl), BF16),
        vm((nz, gr, ff), F32),
        vm((nz, gr, ff), BF16),
        vm((nz, 2, gr, bl), BF16),
        vm((nz, 2, gr, bl), BF16),
        vm((nz - 1, 2, gr, bl), BF16),
        vm((nz - 1, 2, gr, bl), BF16),
        vm((2, gr, bl), BF16),
        vm((3, 2, q, bl), BF16),
        vm((3, 2, q, bl), BF16),
        vm((ny, q, bl), F32),
        vm((ny, q, bl), BF16),
        vm((groups, 8, hb + 2 * patch), BF16),
        vm((groups, 8, hb + 2 * patch), BF16),
        vm((patch, cap), F32),
        vm((patch, cap), F32),
        dma((groups - 1,)),
        dma((groups - 1,)),
        dma((groups - 1,)),
        dma((groups - 1,)),
        dma((2, 3)),
        dma((2, 3)),
        dma((2, 4)),
        dma((2, 4)),
        dma((4,)),
        dma((3,)),
        dma((3,)),
        dma((nz - 1, 2)),
        dma((nz - 1, 2)),
        dma((nz,)),
        dma((nz,)),
        dma((nz, 2)),
        dma((nz, 2)),
        dma((nz - 1, 2)),
        dma((nz - 1, 2)),
        dma((3, 2)),
        dma((3, 2)),
        dma((1,)),
        dma((1,)),
    ]
    hbm = pl.BlockSpec(memory_space=pltpu.HBM)
    smem = pl.BlockSpec(memory_space=pltpu.SMEM)
    vmem = pl.BlockSpec(memory_space=pltpu.VMEM)
    layer_out, clean = pl.pallas_call(
        functools.partial(body, sizes),
        out_shape=(
            jax.ShapeDtypeStruct((cap, bl), BF16),
            jax.ShapeDtypeStruct((patch, cap), F32),
        ),
        in_specs=[smem, smem, vmem, vmem, vmem, hbm, hbm, hbm, hbm],
        out_specs=(vmem, vmem),
        scratch_shapes=scratch,
        compiler_params=pltpu.CompilerParams(
            collective_id=0, has_side_effects=True, vmem_limit_bytes=48 * 1024 * 1024
        ),
    )(
        split_table,
        timestep,
        hidden[0],
        latent.T,
        jnp.asarray(alpha_table()),
        modulation,
        w1,
        w2,
        ow.T,
    )
    return (layer_out[None], clean.T)


def solution(mesh):
    return jax.shard_map(
        functools.partial(on_device, mesh.shape["wide"], mesh.shape["narrow"]),
        mesh=mesh,
        in_specs=(
            P("cfg", "wide", "narrow"),
            P(),
            P(None, "narrow"),
            P("narrow", "wide"),
            P("wide", "narrow"),
            P("narrow", None),
            P("wide", None),
            P(),
        ),
        out_specs=(P("cfg", "wide", "narrow"), P("wide", None)),
        check_vma=False,
    )
```

time: 122 us -> 112 us (0.918)
  Pallas kernels: 114 us -> 102 us
  local copies, waits for them, and re-layouts: 5.12 us -> 7.39 us
    pallas_call x1, Pallas kernels: 114 us -> 102 us  [on_device(): pl.pallas_call(functools.partial(body, sizes), out_shape=(jax.ShapeDtypeS...]
    unnamed x18, local copies, waits for them, and re-layouts: 5.12 us -> 7.39 us
where the time goes in v2:
time: 112 us; the launch traced here: 111 us
  Pallas kernels  102 us (91%)
  local copies, waits for them, and re-layouts  7.39 us (7%)
  between operations  1.32 us (1%)
    pallas_call x1, Pallas kernels, on_device(): pl.pallas_call(functools.partial(body, sizes), out_shape=(jax.ShapeDtypeS...  102 us
    unnamed x18, local copies, waits for them, and re-layouts  7.39 us

profile of v2, /device:TPU:2, one launch (start us, length us, event | category | flops | bytes accessed | tf_op | source)
XLA Modules:
  0.0 110.8 jit_solution(9362739922300205102)
XLA Ops:
  0.6 0.0 copy-start.6
  1.3 0.0 copy-start.7
  1.3 0.0 copy-done.6
  1.3 0.6 copy-done.7
  2.0 0.0 copy-start
  2.0 1.1 copy-done
  3.0 0.0 copy-start.1
  3.0 1.1 copy-done.1
  4.1 0.0 copy-start.2
  4.1 0.9 copy-done.2
  5.0 0.0 copy-start.3
  5.0 0.9 copy-done.3
  5.9 0.0 copy-start.4
  5.9 0.8 copy-done.4
  6.7 0.0 copy-start.5
  6.7 0.7 copy-done.5
  7.4 102.1 %shard_map.104 = (bf16[128,768]{1,0:T(8,128)(2,1)S(1)}, f32[64,128]{1,0:T(8,128)S(1)}) custom-call(s32[32]{0:T(128)S(1)} %copy-done.7, s32[1]{0:T(128)S(6)} %copy.13.time_ref, bf16[128,768]{1,0:T(8,128)(2,1)S(1)} %bitcast.6, f32[64,128]{1,0:T(8,128)S(1)} %bitcast.9, f32[8,128]{1,0:T(8,128)S(1)} %copy-done.6, f32[8,768]{1,0:T(8,128)S(1)} %copy-done.5, ...), custom_call_target="tpu_custom_call" | custom-call | tf_op jit(solution)/shard_map/pallas_call | solution.py:602
  109.6 0.7 copy.14
  110.2 0.6 copy.15
Async XLA Ops:
  0.6 0.7 copy-start.6
  1.3 0.7 copy-start.7
  2.0 1.1 copy-start
  3.0 1.1 copy-start.1
  4.1 0.9 copy-start.2
  5.0 0.9 copy-start.3
  5.9 0.8 copy-start.4
  6.7 0.7 copy-start.5

commit v3 on v2

--- a/solution.py
+++ b/solution.py
@@ -56,6 +56,7 @@
     out_ref,
     clean_ref,
     slab_s,
+    slab_y,
     slab_r,
     xr,
     modg,
@@ -78,13 +79,18 @@
     ffb,
     lo,
     back_s,
+    back_z,
     back_r,
     vel_s,
     vel_r,
     a_s,
     a_r,
+    az_s,
+    az_r,
     b_s,
     b_r,
+    bz_s,
+    bz_r,
     y_s,
     y_r,
     w_s,
@@ -137,15 +143,8 @@
     def ypeer(k):
         return (cfg, w, yid(k))
 
-    def peer(k):
-        m = lax.rem(n + k // nz, ny)
-        zd = lax.rem(z + lax.rem(k, nz), nz)
-        return m * nz + zd, (cfg, wide_of(xh, zd, core), m)
-
-    def source(k):
-        m = lax.rem(n + ny - k // nz, ny)
-        zd = lax.rem(z + nz - lax.rem(k, nz), nz)
-        return m * nz + zd
+    def zpeer(k):
+        return (cfg, wide_of(xh, zmod(z + k), core), n)
 
     def rcopy(src, dst, ssem, rsem, dev):
         return pltpu.make_async_remote_copy(
@@ -169,9 +168,9 @@
         lax.fori_loop(first, count, step, 0)
 
     barrier = pltpu.get_barrier_semaphore()
-    times(groups, lambda k: signal(peer(k)[1]), 1)
-    for dev in (sib, xpart, diag, cpart):
+    for dev in (ypeer(1), ypeer(2), ypeer(3), sib, xpart, diag, cpart):
         signal(dev)
+    times(nz, lambda k: signal(zpeer(k)), 1)
 
     own = [(mod_ref, modg.at[n]), (w1_ref, w1g.at[n]), (w2_ref, w2g.at[n]), (ow_ref, owg.at[n])]
     for i, (src, dst) in enumerate(own):
@@ -191,17 +190,14 @@
     hit = residue == ((iota((groups * 8, cap), 1) + offset) & (cap - 1))
     low = (row & 4) == 0
     slabs = dot(one_hot(hit & low), hidden_ref[:, :hb]) + dot(one_hot(hit & ~low), hidden_ref[:, hb:])
-    slab_s[...] = slabs.reshape(groups, 8, hb).astype(BF16)
-    pl.semaphore_wait(barrier, groups - 1 + 4)
-
-    def slab_out(k):
-        target, dev = peer(k)
-        rcopy(slab_s.at[target], slab_r.at[n * nz + z], a_s.at[k - 1], a_r.at[k - 1], dev).start()
-
-    times(groups, slab_out, 1)
+    slab_s[...] = slabs.reshape(ny, nz, 8, hb).astype(BF16)
+    pl.semaphore_wait(barrier, 7 + nz - 1)
+
+    for k in (1, 3, 2):
+        rcopy(slab_s.at[yid(k)], slab_y.at[n], a_s.at[k - 1], a_r.at[k - 1], ypeer(k)).start()
     for k in (1, 3, 2):
         rcopy(mod_ref, modg.at[n], y_s.at[0, k - 1], y_r.at[0, k - 1], ypeer(k)).start()
-    slab_r[n * nz + z] = slab_s[n * nz + z]
+    slab_y[n] = slab_s[n]
     weights = [(w1_ref, w1g, bl // 2), (w2_ref, w2g, ff // 2)]
 
     def weight_out(i):
@@ -225,8 +221,19 @@
         arrived(dst.at[yid(2), pl.ds(part, part), :], w_r.at[i, 3])
 
     weight_out(0)
+    for k in (1, 2, 3):
+        arrived(slab_y.at[yid(ny - k)], a_r.at[k - 1])
+
+    def slab_on(k):
+        zt = zmod(z + k)
+        rcopy(slab_y.at[:, zt], slab_r.at[:, z], az_s.at[k - 1], az_r.at[k - 1], zpeer(k)).start()
+
+    times(nz, slab_on, 1)
+    weight_out(1)
     for k in (1, 3, 2):
         rcopy(ow_ref, owg.at[n], y_s.at[1, k - 1], y_r.at[1, k - 1], ypeer(k)).start()
+    for b in range(ny):
+        slab_r[b, z] = slab_y[b, z]
     hid[...] = jnp.zeros_like(hid)
 
     def slot_table(shape, dim):
@@ -273,11 +280,11 @@
     unlow = (uncol & 4) == 0
     take_low = one_hot(unhit & unlow)
     take_high = one_hot(unhit & ~unlow)
-    times(groups, lambda k: arrived(slab_r.at[source(k)], a_r.at[k - 1]), 1)
+    times(nz, lambda k: arrived(slab_r.at[:, zmod(z - k)], az_r.at[k - 1]), 1)
     total = jnp.zeros((q, 1), F32)
     squares = jnp.zeros((q, 1), F32)
     for b in range(ny):
-        v = slab_r[b * nz : (b + 1) * nz].astype(F32).reshape(nz * 8, hb).astype(BF16)
+        v = slab_r[b].astype(F32).reshape(nz * 8, hb).astype(BF16)
         for part, take in ((0, take_low), (1, take_high)):
             u = dot(take, v)
             xr[b, :, part * hb : (part + 1) * hb] = u.astype(BF16)
@@ -300,6 +307,7 @@
         rcopy(nst.at[pl.ds(blk, 2)], gx.at[:, own_rows, :], e_s.at[i], e_r.at[i], dev).start()
     for j in range(2):
         gx[j, own_rows, :] = nst[mine + j]
+    weight_on(0)
     for i in range(3):
         arrived(gx.at[:, rows_of(mates[i][1], q), :], e_r.at[i])
     for j in range(2):
@@ -338,10 +346,8 @@
         share(-s)
         if 0 < s <= lb:
             share(s)
-        if s == min(1, la - 1):
-            weight_on(0)
-            weight_out(1)
         if s == la - 1:
+            weight_on(1)
             weight_in(0)
             work(0)
 
@@ -357,7 +363,6 @@
         for j in range(2):
             arrived(xa.at[zmod(z + d * s), mine + j], ag_r.at[la + s - 1, j])
         share(s)
-    weight_on(1)
     for u in range(la, nz - la + 1):
         work(u)
     times(nz, gelu)
@@ -467,15 +472,16 @@
     terms = dot(put_low, jnp.concatenate([coarse, fine], axis=1)).reshape(nz, 8, 2 * patch).astype(BF16)
     for b in range(ny):
         v = dot(put_low, lo[b, :, :hb]) + dot(put_high, lo[b, :, hb:])
-        back_s[b * nz : (b + 1) * nz, :, :hb] = v.reshape(nz, 8, hb).astype(BF16)
-        back_s[b * nz : (b + 1) * nz, :, hb:] = terms
+        back_s[b, :, :, :hb] = v.reshape(nz, 8, hb).astype(BF16)
+        back_s[b, :, :, hb:] = terms
 
     def back_out(k):
-        target, dev = peer(k)
-        rcopy(back_s.at[target], back_r.at[n * nz + z], b_s.at[k - 1], b_r.at[k - 1], dev).start()
-
-    times(groups, back_out, 1)
-    back_r[n * nz + z] = back_s[n * nz + z]
+        zt = zmod(z + k)
+        rcopy(back_s.at[:, zt], back_z.at[:, z], bz_s.at[k - 1], bz_r.at[k - 1], zpeer(k)).start()
+
+    times(nz, back_out, 1)
+    for b in range(ny):
+        back_z[b, z] = back_s[b, z]
 
     column = iota((cap, groups * 8), 1)
     undo = ((column >> 3) * 4 + (column & 3)) == ((iota((cap, groups * 8), 0) + offset) & (cap - 1))
@@ -488,22 +494,29 @@
     factor = jnp.sqrt(1.0 - alpha)
     lanes = iota((1, cap), 1)
     video = (lanes < count) & (lanes + offset >= TEXT)
-    times(groups, lambda k: arrived(back_r.at[source(k)], b_r.at[k - 1]), 1)
-    v = back_r[:, :, hb:].astype(F32).reshape(groups * 8, 2 * patch).astype(BF16)
+    times(nz, lambda k: arrived(back_z.at[:, zmod(z - k)], bz_r.at[k - 1]), 1)
+    for k in (1, 3, 2):
+        rcopy(back_z.at[yid(k)], back_r.at[n], b_s.at[k - 1], b_r.at[k - 1], ypeer(k)).start()
+    back_r[n] = back_z[n]
+    for k in (1, 2, 3):
+        arrived(back_r.at[yid(ny - k)], b_r.at[k - 1])
+    v = back_r[:, :, :, hb:].astype(F32).reshape(groups * 8, 2 * patch).astype(BF16)
     v = dot(undo_low, v).T
     vel_s[...] = v[:patch] + v[patch:]
     rcopy(vel_s, vel_r, c_s.at[0], c_r.at[0], cpart).start()
-    v = back_r[:, :, :hb].astype(F32).reshape(groups * 8, hb).astype(BF16)
+    v = back_r[:, :, :, :hb].astype(F32).reshape(groups * 8, hb).astype(BF16)
     out_ref[:, :hb] = dot(undo_low, v).astype(BF16)
     out_ref[:, hb:] = dot(undo_high, v).astype(BF16)
 
     def slabs_sent(k):
-        target = peer(k)[0]
-        sent(slab_s.at[target], a_s.at[k - 1])
-        sent(back_s.at[target], b_s.at[k - 1])
-
-    times(groups, slabs_sent, 1)
+        zt = zmod(z + k)
+        sent(slab_y.at[:, zt], az_s.at[k - 1])
+        sent(back_s.at[:, zt], bz_s.at[k - 1])
+
+    times(nz, slabs_sent, 1)
     for k in (1, 2, 3):
+        sent(slab_s.at[yid(k)], a_s.at[k - 1])
+        sent(back_z.at[yid(k)], b_s.at[k - 1])
         sent(mod_ref, y_s.at[0, k - 1])
         sent(ow_ref, y_s.at[1, k - 1])
     for i, (src, dst, part) in enumerate(weights):
@@ -541,13 +554,13 @@
     q = cap // ny
     gr = n_wide * 2
     sizes = (nz, ny, q, gr, bl, ff, cap, patch)
-    groups = ny * nz
     hb = bl // 2
     dma = pltpu.SemaphoreType.DMA
     vm = pltpu.VMEM
     scratch = [
-        vm((groups, 8, hb), BF16),
-        vm((groups, 8, hb), BF16),
+        vm((ny, nz, 8, hb), BF16),
+        vm((ny, nz, 8, hb), BF16),
+        vm((ny, nz, 8, hb), BF16),
         vm((ny, q, bl), BF16),
         vm((ny, 8, bl), F32),
         vm((ny, patch, bl), BF16),
@@ -568,14 +581,19 @@
         vm((3, 2, q, bl), BF16),
         vm((ny, q, bl), F32),
         vm((ny, q, bl), BF16),
-        vm((groups, 8, hb + 2 * patch), BF16),
-        vm((groups, 8, hb + 2 * patch), BF16),
+        vm((ny, nz, 8, hb + 2 * patch), BF16),
+        vm((ny, nz, 8, hb + 2 * patch), BF16),
+        vm((ny, nz, 8, hb + 2 * patch), BF16),
         vm((patch, cap), F32),
         vm((patch, cap), F32),
-        dma((groups - 1,)),
-        dma((groups - 1,)),
-        dma((groups - 1,)),
-        dma((groups - 1,)),
+        dma((ny - 1,)),
+        dma((ny - 1,)),
+        dma((nz - 1,)),
+        dma((nz - 1,)),
+        dma((ny - 1,)),
+        dma((ny - 1,)),
+        dma((nz - 1,)),
+        dma((nz - 1,)),
         dma((2, 3)),
         dma((2, 3)),
         dma((2, 4)),
@@ -609,7 +627,7 @@
         out_specs=(vmem, vmem),
         scratch_shapes=scratch,
         compiler_params=pltpu.CompilerParams(
-            collective_id=0, has_side_effects=True, vmem_limit_bytes=48 * 1024 * 1024
+            collective_id=0, has_side_effects=True, vmem_limit_bytes=60 * 1024 * 1024
         ),
     )(
         split_table,

time: 112 us -> 115 us (1.027)
  Pallas kernels: 102 us -> 111 us
  local copies, waits for them, and re-layouts: 7.39 us -> 2.24 us
    pallas_call x1, Pallas kernels: 102 us -> 111 us  [on_device(): pl.pallas_call(functools.partial(body, sizes), out_shape=(jax.ShapeDtypeS...]
    unnamed x18 -> x4, local copies, waits for them, and re-layouts: 7.39 us -> 2.24 us
where the time goes in v3:
time: 115 us
  Pallas kernels  111 us (97%)
  local copies, waits for them, and re-layouts  2.24 us (2%)
  between operations  1.3 us (1%)
    pallas_call x1, Pallas kernels, on_device(): pl.pallas_call(functools.partial(body, sizes), out_shape=(jax.ShapeDtypeS...  111 us

profile of v3, /device:TPU:2, one launch (start us, length us, event | category | flops | bytes accessed | tf_op | source)
XLA Modules:
  0.0 114.9 jit_solution(13803495792952774864)
XLA Ops:
  1.3 111.4 %shard_map.104 = (bf16[128,768]{1,0:T(8,128)(2,1)}, f32[64,128]{1,0:T(8,128)}) custom-call(s32[32]{0:T(128)} %split_ref.1, s32[1]{0:T(128)S(6)} %copy.13.time_ref, bf16[128,768]{1,0:T(8,128)(2,1)} %bitcast.6, f32[64,128]{1,0:T(8,128)} %bitcast.9, f32[8,128]{1,0:T(8,128)} %constant.2.clone.alpha_ref, f32[8,768]{1,0:T(8,128)} %mod_ref.1, ...), custom_call_target="tpu_custom_call" | custom-call | tf_op jit(solution)/shard_map/pallas_call | solution.py:620
  112.7 0.0 copy-start
  112.7 1.6 %copy.14 = bf16[1,128,768]{2,1,0:T(8,128)(2,1)} copy(bf16[1,128,768]{2,1,0:T(8,128)(2,1)} %bitcast.5) | data formatting | bytes 393216
  114.3 0.0 copy-done
  114.3 0.6 copy.15
Async XLA Ops:
  112.7 1.6 %copy-start = (f32[64,128]{1,0:T(8,128)S(1)}, f32[64,128]{1,0:T(8,128)}, u32[]{:S(2)}) copy-start(f32[64,128]{1,0:T(8,128)} %get-tuple-element.5) | copy-start | bytes 98308

commit v4 on v2

--- a/solution.py
+++ b/solution.py
@@ -202,27 +202,63 @@
     for k in (1, 3, 2):
         rcopy(mod_ref, modg.at[n], y_s.at[0, k - 1], y_r.at[0, k - 1], ypeer(k)).start()
     slab_r[n * nz + z] = slab_s[n * nz + z]
-    weights = [(w1_ref, w1g, bl // 2), (w2_ref, w2g, ff // 2)]
+    weights = [(w1_ref, w1g, bl // 4), (w2_ref, w2g, ff // 4)]
+    give, far_own = 3 * cfg, 2 * cfg
+
+    def rows_at(i, first, quarters):
+        part = weights[i][2]
+        return pl.ds(pl.multiple_of(first * part, part), quarters * part)
+
+    def piece(i, blk, first, quarters):
+        return weights[i][1].at[blk, rows_at(i, first, quarters), :]
+
+    sides = ((yid(3), ypeer(1)), (yid(1), ypeer(3)))
+
+    def pass_on(i, blk, first, quarters, sem, dev):
+        rcopy(piece(i, blk, first, quarters), piece(i, blk, first, quarters), w_s.at[i, sem], w_r.at[i, sem], dev).start()
 
     def weight_out(i):
-        src, dst, _ = weights[i]
-        rcopy(src, dst.at[n], w_s.at[i, 0], w_r.at[i, 0], ypeer(1)).start()
-        rcopy(src, dst.at[n], w_s.at[i, 1], w_r.at[i, 1], ypeer(3)).start()
+        src = weights[i][0]
+        for sem, first, quarters in ((0, give, 1), (2, 1, 2)):
+            for k in range(2):
+                rcopy(
+                    src.at[rows_at(i, first, quarters), :],
+                    piece(i, n, first, quarters),
+                    w_s.at[i, sem + k],
+                    w_r.at[i, sem + k],
+                    sides[k][1],
+                ).start()
+
+    def weight_give(i):
+        for k in range(2):
+            arrived(piece(i, sides[k][0], give, 1), w_r.at[i, k])
+            pass_on(i, sides[k][0], give, 1, 4 + k, cpart)
 
     def weight_on(i):
-        _, dst, part = weights[i]
+        for k in range(2):
+            arrived(piece(i, sides[k][0], 1, 2), w_r.at[i, 2 + k])
+            pass_on(i, sides[k][0], far_own + k, 1, 6 + k, sides[k][1])
+
+    def weight_far(i):
+        for k in range(2):
+            arrived(piece(i, yid(2), far_own + k, 1), w_r.at[i, 6 + k])
+        pass_on(i, yid(2), far_own, 2, 8, cpart)
+
+    def weight_near_in(i):
         pltpu.make_async_copy(own[1 + i][0], own[1 + i][1], loc.at[1 + i]).wait()
-        arrived(dst.at[yid(3)], w_r.at[i, 0])
-        first = dst.at[yid(3), pl.ds(0, part), :]
-        rcopy(first, first, w_s.at[i, 2], w_r.at[i, 2], ypeer(1)).start()
-        arrived(dst.at[yid(1)], w_r.at[i, 1])
-        second = dst.at[yid(1), pl.ds(part, part), :]
-        rcopy(second, second, w_s.at[i, 3], w_r.at[i, 3], ypeer(3)).start()
-
-    def weight_in(i):
-        _, dst, part = weights[i]
-        arrived(dst.at[yid(2), pl.ds(0, part), :], w_r.at[i, 2])
-        arrived(dst.at[yid(2), pl.ds(part, part), :], w_r.at[i, 3])
+        for k in range(2):
+            arrived(piece(i, sides[k][0], 3 - give, 1), w_r.at[i, 4 + k])
+
+    def weight_far_in(i):
+        arrived(piece(i, yid(2), 2 - far_own, 2), w_r.at[i, 8])
+
+    def weights_sent(i):
+        for k in range(2):
+            sent(weights[i][0].at[rows_at(i, give, 1), :], w_s.at[i, k])
+            sent(weights[i][0].at[rows_at(i, 1, 2), :], w_s.at[i, 2 + k])
+            sent(piece(i, sides[k][0], give, 1), w_s.at[i, 4 + k])
+            sent(piece(i, sides[k][0], far_own + k, 1), w_s.at[i, 6 + k])
+        sent(piece(i, yid(2), far_own, 2), w_s.at[i, 8])
 
     weight_out(0)
     for k in (1, 3, 2):
@@ -273,6 +309,7 @@
     unlow = (uncol & 4) == 0
     take_low = one_hot(unhit & unlow)
     take_high = one_hot(unhit & ~unlow)
+    weight_give(0)
     times(groups, lambda k: arrived(slab_r.at[source(k)], a_r.at[k - 1]), 1)
     total = jnp.zeros((q, 1), F32)
     squares = jnp.zeros((q, 1), F32)
@@ -300,6 +337,8 @@
         rcopy(nst.at[pl.ds(blk, 2)], gx.at[:, own_rows, :], e_s.at[i], e_r.at[i], dev).start()
     for j in range(2):
         gx[j, own_rows, :] = nst[mine + j]
+    weight_on(0)
+    weight_out(1)
     for i in range(3):
         arrived(gx.at[:, rows_of(mates[i][1], q), :], e_r.at[i])
     for j in range(2):
@@ -326,6 +365,7 @@
         v = hid[o]
         act[o] = (0.5 * v * (1.0 + jnp.tanh(0.7978845608 * (v + 0.044715 * (v * v * v))))).astype(BF16)
 
+    plan = ((0, weight_far, 0), (1, weight_give, 1), (2, weight_on, 1), (3, weight_far, 1))
     for s in range(la):
         for j in range(2):
             if s > 0:
@@ -338,11 +378,12 @@
         share(-s)
         if 0 < s <= lb:
             share(s)
-        if s == min(1, la - 1):
-            weight_on(0)
-            weight_out(1)
+        for at, action, i in plan:
+            if s == min(at, la - 1):
+                action(i)
         if s == la - 1:
-            weight_in(0)
+            weight_near_in(0)
+            weight_far_in(0)
             work(0)
 
             def pair(k):
@@ -357,7 +398,6 @@
         for j in range(2):
             arrived(xa.at[zmod(z + d * s), mine + j], ag_r.at[la + s - 1, j])
         share(s)
-    weight_on(1)
     for u in range(la, nz - la + 1):
         work(u)
     times(nz, gelu)
@@ -410,7 +450,7 @@
     stages = {}
     for t, (kind, s, _) in enumerate(order):
         stages.setdefault(la if kind == "stay" else s, []).append(t)
-    lag = 2
+    lag = 0
     events = []
     for step in range(la + 1 + lag):
         for b in range(2):
@@ -418,13 +458,14 @@
             if 0 <= at <= la:
                 events += [(t, b) for t in stages[at]]
     ahead = 2
+    weight_near_in(1)
     for t, b in events[:ahead]:
         sib_part(t, b)
     needs_far = False
     for i, (t, b) in enumerate(events):
         if i + ahead < len(events):
             if events[i + ahead][1] == 1 and not needs_far:
-                weight_in(1)
+                weight_far_in(1)
                 needs_far = True
             sib_part(*events[i + ahead])
         ring_part(t, b)
@@ -506,11 +547,8 @@
     for k in (1, 2, 3):
         sent(mod_ref, y_s.at[0, k - 1])
         sent(ow_ref, y_s.at[1, k - 1])
-    for i, (src, dst, part) in enumerate(weights):
-        sent(src, w_s.at[i, 0])
-        sent(src, w_s.at[i, 1])
-        sent(dst.at[yid(3), pl.ds(0, part), :], w_s.at[i, 2])
-        sent(dst.at[yid(1), pl.ds(part, part), :], w_s.at[i, 3])
+    for i in range(2):
+        weights_sent(i)
     for i in range(3):
         sent(nst.at[pl.ds(mates[i][2], 2)], e_s.at[i])
         for b in range(2):
@@ -578,8 +616,8 @@
         dma((groups - 1,)),
         dma((2, 3)),
         dma((2, 3)),
-        dma((2, 4)),
-        dma((2, 4)),
+        dma((2, 9)),
+        dma((2, 9)),
         dma((4,)),
         dma((3,)),
         dma((3,)),
@@ -609,7 +647,7 @@
         out_specs=(vmem, vmem),
         scratch_shapes=scratch,
         compiler_params=pltpu.CompilerParams(
-            collective_id=0, has_side_effects=True, vmem_limit_bytes=48 * 1024 * 1024
+            collective_id=0, has_side_effects=True, vmem_limit_bytes=60 * 1024 * 1024
         ),
     )(
         split_table,

time: 112 us -> 101 us (0.902)
  local copies, waits for them, and re-layouts: 7.39 us -> 2.24 us
  Pallas kernels: 102 us -> 97.2 us
    unnamed x18 -> x4, local copies, waits for them, and re-layouts: 7.39 us -> 2.24 us
    pallas_call x1, Pallas kernels: 102 us -> 97.2 us  [on_device(): pl.pallas_call(functools.partial(body, sizes), out_shape=(jax.ShapeDtypeS...]
where the time goes in v4:
time: 101 us
  Pallas kernels  97.2 us (96%)
  local copies, waits for them, and re-layouts  2.24 us (2%)
  between operations  1.3 us (1%)
    pallas_call x1, Pallas kernels, on_device(): pl.pallas_call(functools.partial(body, sizes), out_shape=(jax.ShapeDtypeS...  97.2 us
    unnamed x4, local copies, waits for them, and re-layouts  2.24 us

profile of v4, /device:TPU:2, one launch (start us, length us, event | category | flops | bytes accessed | tf_op | source)
XLA Modules:
  0.0 100.8 jit_solution(8403728948733622996)
XLA Ops:
  1.3 97.2 %shard_map.104 = (bf16[128,768]{1,0:T(8,128)(2,1)}, f32[64,128]{1,0:T(8,128)}) custom-call(s32[32]{0:T(128)} %split_ref.1, s32[1]{0:T(128)S(6)} %copy.13.time_ref, bf16[128,768]{1,0:T(8,128)(2,1)} %bitcast.6, f32[64,128]{1,0:T(8,128)} %bitcast.9, f32[8,128]{1,0:T(8,128)} %constant.2.clone.alpha_ref, f32[8,768]{1,0:T(8,128)} %mod_ref.1, ...), custom_call_target="tpu_custom_call" | custom-call | tf_op jit(solution)/shard_map/pallas_call | solution.py:640
  98.5 0.0 copy-start
  98.5 1.6 %copy.14 = bf16[1,128,768]{2,1,0:T(8,128)(2,1)} copy(bf16[1,128,768]{2,1,0:T(8,128)(2,1)} %bitcast.5) | data formatting | bytes 393216
  100.1 0.0 copy-done
  100.1 0.6 copy.15
Async XLA Ops:
  98.5 1.6 %copy-start = (f32[64,128]{1,0:T(8,128)S(1)}, f32[64,128]{1,0:T(8,128)}, u32[]{:S(2)}) copy-start(f32[64,128]{1,0:T(8,128)} %get-tuple-element.5) | copy-start | bytes 98308

commit v5 on v4

--- a/solution.py
+++ b/solution.py
@@ -497,18 +497,23 @@
         velocity = velocity + dot_nt(v, owg[b])
     velocity = velocity * jnp.where(cfg == 0, GUIDANCE, 1.0 - GUIDANCE)
 
-    coarse = velocity.astype(BF16)
-    fine = (velocity - coarse.astype(F32)).astype(BF16)
+    vel_s[...] = velocity
+    rcopy(vel_s, vel_r, c_s.at[0], c_r.at[0], cpart).start()
     backrow = iota((2 * q, q), 0)
     backcol = iota((2 * q, q), 1)
     backhit = ((backcol >> 2) == (backrow >> 3)) & ((backcol & 3) == (backrow & 3))
     backlow = (backrow & 4) == 0
     put_low = one_hot(backhit & backlow)
     put_high = one_hot(backhit & ~backlow)
-    terms = dot(put_low, jnp.concatenate([coarse, fine], axis=1)).reshape(nz, 8, 2 * patch).astype(BF16)
     for b in range(ny):
         v = dot(put_low, lo[b, :, :hb]) + dot(put_high, lo[b, :, hb:])
         back_s[b * nz : (b + 1) * nz, :, :hb] = v.reshape(nz, 8, hb).astype(BF16)
+    arrived(vel_r, c_r.at[0])
+    guided = vel_s[...] + vel_r[...]
+    coarse = guided.astype(BF16)
+    fine = (guided - coarse.astype(F32)).astype(BF16)
+    terms = dot(put_low, jnp.concatenate([coarse, fine], axis=1)).reshape(nz, 8, 2 * patch).astype(BF16)
+    for b in range(ny):
         back_s[b * nz : (b + 1) * nz, :, hb:] = terms
 
     def back_out(k):
@@ -532,8 +537,7 @@
     times(groups, lambda k: arrived(back_r.at[source(k)], b_r.at[k - 1]), 1)
     v = back_r[:, :, hb:].astype(F32).reshape(groups * 8, 2 * patch).astype(BF16)
     v = dot(undo_low, v).T
-    vel_s[...] = v[:patch] + v[patch:]
-    rcopy(vel_s, vel_r, c_s.at[0], c_r.at[0], cpart).start()
+    clean_ref[...] = jnp.where(video, scaled - factor * (v[:patch] + v[patch:]), 0.0)
     v = back_r[:, :, :hb].astype(F32).reshape(groups * 8, hb).astype(BF16)
     out_ref[:, :hb] = dot(undo_low, v).astype(BF16)
     out_ref[:, hb:] = dot(undo_high, v).astype(BF16)
@@ -565,8 +569,6 @@
             sent(sib_s.at[t, b], pr_s.at[t, b])
             if t < nz - 1:
                 sent(ring_s.at[t, b], rg_s.at[t, b])
-    arrived(vel_r, c_r.at[0])
-    clean_ref[...] = jnp.where(video, scaled - factor * (vel_s[...] + vel_r[...]), 0.0)
     sent(vel_s, c_s.at[0])
 
 
@@ -608,8 +610,8 @@
         vm((ny, q, bl), BF16),
         vm((groups, 8, hb + 2 * patch), BF16),
         vm((groups, 8, hb + 2 * patch), BF16),
-        vm((patch, cap), F32),
-        vm((patch, cap), F32),
+        vm((q, patch), F32),
+        vm((q, patch), F32),
         dma((groups - 1,)),
         dma((groups - 1,)),
         dma((groups - 1,)),

time: 101 us -> 100 us (0.990)
  no operation moved by 1% of the time
where the time goes in v5:
time: 100 us; the launch traced here: 99.9 us
  Pallas kernels  96.4 us (96%)
  local copies, waits for them, and re-layouts  2.24 us (2%)
  between operations  1.3 us (1%)
    pallas_call x1, Pallas kernels, on_device(): pl.pallas_call(functools.partial(body, sizes), out_shape=(jax.ShapeDtypeS...  96.4 us
    unnamed x4, local copies, waits for them, and re-layouts  2.24 us

profile of v5, /device:TPU:2, one launch (start us, length us, event | category | flops | bytes accessed | tf_op | source)
XLA Modules:
  0.0 99.9 jit_solution(4963948486949843864)
XLA Ops:
  1.3 96.4 %shard_map.104 = (bf16[128,768]{1,0:T(8,128)(2,1)}, f32[64,128]{1,0:T(8,128)}) custom-call(s32[32]{0:T(128)} %split_ref.1, s32[1]{0:T(128)S(6)} %copy.13.time_ref, bf16[128,768]{1,0:T(8,128)(2,1)} %bitcast.6, f32[64,128]{1,0:T(8,128)} %bitcast.9, f32[8,128]{1,0:T(8,128)} %constant.2.clone.alpha_ref, f32[8,768]{1,0:T(8,128)} %mod_ref.1, ...), custom_call_target="tpu_custom_call" | custom-call | tf_op jit(solution)/shard_map/pallas_call | solution.py:642
  97.7 0.0 copy-start
  97.7 1.6 %copy.14 = bf16[1,128,768]{2,1,0:T(8,128)(2,1)} copy(bf16[1,128,768]{2,1,0:T(8,128)(2,1)} %bitcast.5) | data formatting | bytes 393216
  99.3 0.0 copy-done
  99.3 0.6 copy.15
Async XLA Ops:
  97.7 1.6 %copy-start = (f32[64,128]{1,0:T(8,128)S(1)}, f32[64,128]{1,0:T(8,128)}, u32[]{:S(2)}) copy-start(f32[64,128]{1,0:T(8,128)} %get-tuple-element.5) | copy-start | bytes 98308

commit v6 on v5

--- a/solution.py
+++ b/solution.py
@@ -311,6 +311,7 @@
     take_high = one_hot(unhit & ~unlow)
     weight_give(0)
     times(groups, lambda k: arrived(slab_r.at[source(k)], a_r.at[k - 1]), 1)
+    weight_out(1)
     total = jnp.zeros((q, 1), F32)
     squares = jnp.zeros((q, 1), F32)
     for b in range(ny):
@@ -338,7 +339,6 @@
     for j in range(2):
         gx[j, own_rows, :] = nst[mine + j]
     weight_on(0)
-    weight_out(1)
     for i in range(3):
         arrived(gx.at[:, rows_of(mates[i][1], q), :], e_r.at[i])
     for j in range(2):

time: 100 us -> 107 us (1.070)
  Pallas kernels: 96.4 us -> 104 us
    pallas_call x1, Pallas kernels: 96.4 us -> 104 us  [on_device(): pl.pallas_call(functools.partial(body, sizes), out_shape=(jax.ShapeDtypeS...]
where the time goes in v6:
time: 107 us
  Pallas kernels  104 us (97%)
  local copies, waits for them, and re-layouts  2.24 us (2%)
  between operations  1.3 us (1%)
    pallas_call x1, Pallas kernels, on_device(): pl.pallas_call(functools.partial(body, sizes), out_shape=(jax.ShapeDtypeS...  104 us
    unnamed x4, local copies, waits for them, and re-layouts  2.24 us

profile of v6, /device:TPU:2, one launch (start us, length us, event | category | flops | bytes accessed | tf_op | source)
XLA Modules:
  0.0 107.4 jit_solution(3733656249009617943)
XLA Ops:
  1.3 103.8 %shard_map.104 = (bf16[128,768]{1,0:T(8,128)(2,1)}, f32[64,128]{1,0:T(8,128)}) custom-call(s32[32]{0:T(128)} %split_ref.1, s32[1]{0:T(128)S(6)} %copy.13.time_ref, bf16[128,768]{1,0:T(8,128)(2,1)} %bitcast.6, f32[64,128]{1,0:T(8,128)} %bitcast.9, f32[8,128]{1,0:T(8,128)} %constant.2.clone.alpha_ref, f32[8,768]{1,0:T(8,128)} %mod_ref.1, ...), custom_call_target="tpu_custom_call" | custom-call | tf_op jit(solution)/shard_map/pallas_call | solution.py:642
  105.1 0.0 copy-start
  105.1 1.6 %copy.14 = bf16[1,128,768]{2,1,0:T(8,128)(2,1)} copy(bf16[1,128,768]{2,1,0:T(8,128)(2,1)} %bitcast.5) | data formatting | bytes 393216
  106.7 0.0 copy-done
  106.7 0.6 copy.15
Async XLA Ops:
  105.1 1.6 %copy-start = (f32[64,128]{1,0:T(8,128)S(1)}, f32[64,128]{1,0:T(8,128)}, u32[]{:S(2)}) copy-start(f32[64,128]{1,0:T(8,128)} %get-tuple-element.5) | copy-start | bytes 98308
